TPU v7x, 128 devices: a whole 4x4x4 slice. The times are simulated.
128 devices in a mesh: rows: 16 (over z, x), heads: 8 (over y, core).
Axes of the slice: x: 4, y: 4, z: 4, core: 2. Of those that a mesh axis runs over, the one named last changes fastest.
Arguments:
- stream: bfloat16 [256, 4096], P('rows', 'heads'), may hold values from -6 to 6
- self_query: bfloat16 [256, 8192], P('rows', 'heads'), may hold values from -200 to 200
- new_kv: bfloat16 [256, 8, 256], P('rows', 'heads'), may hold values from -8 to 8
- cache_pool: bfloat16 [1536, 64, 8, 256], P('rows', None, 'heads'), may hold values from -8 to 8
- page_table: int32 [256, 6], P('rows'), may hold values from 0 to 95, as said below
- lengths: int32 [256], P('rows'), may hold values from 1 to 383, as said below
- migration: int32 [256, 2], P('rows'), may hold values from -1 to 15, as said below
- image_of: int32 [256], replicated, may hold values from 0 to 15, as said below
- cross_query: bfloat16 [256, 8192], P('rows', 'heads'), may hold values from -200 to 200
- image_cache: bfloat16 [16, 2048, 8, 256], P(None, 'rows', 'heads'), may hold values from -8 to 8
- self_output: bfloat16 [8192, 4096], P('heads'), may hold values from -0.125 to 0.125
- cross_output: bfloat16 [8192, 4096], P('heads'), may hold values from -0.5 to 0.5
- cross_gate: float32 [1], replicated, may hold values from 0.3 to 1.2
Outputs:
- self_update: bfloat16 [256, 4096], P('rows', 'heads')
- cross_update: bfloat16 [256, 4096], P('rows', 'heads')
- new_cache: bfloat16 [256, 384, 8, 256], P('rows', None, 'heads')
Inputs may be any that keep to these rules, and one draw needn't show every extreme that they name: `page_table`: each index of rows lists, over its 16 rows, every page number of its block of 96 pages exactly once. The new token of row r goes to position lengths[r]. `migration`: A finished row gives (-1, -1), a live row (destination index along rows, slot). No slot of a destination is named twice. The slots of a destination form aligned groups of 2, each group named only by rows of one index of rows; the rows of one index go to 8 different destinations, at most 2 rows to each, and some index sends 2 live rows to one destination. Some destination has all 16 slots named. `image_of`: every image is the image of exactly 16 rows.
All inputs are finite; a program needn't handle non-finite values.
Results may differ from a plain program's by a relative error of at most 0.0085.
Values may be sent and summed in bfloat16 or wider, within the bound.
No kernel may reach another device: no remote copies, remote signals or barrier semaphores. Data moves between devices by JAX's collectives and lax.ppermute only.
A program may use at most 128 MiB of HBM per device.

v0:
```python
import functools
import math

import jax
import jax.numpy as jnp
from jax import lax
from jax.experimental import pallas as pl
from jax.experimental.pallas import tpu as pltpu
from jax.sharding import PartitionSpec as P

very_low = -1e30
bf16 = jnp.bfloat16
f32 = jnp.float32
i32 = jnp.int32
LANES = 128
VMEM = pltpu.VMEM
SMEM = pltpu.SMEM


def vmem():
    return pl.BlockSpec(memory_space=VMEM)


def smem():
    return pl.BlockSpec(memory_space=SMEM)


def anywhere():
    return pl.BlockSpec(memory_space=pl.ANY)


def iota(shape, dim):
    return lax.broadcasted_iota(i32, shape, dim)


def onto(a, b):
    return lax.dot_general(a, b, (((0,), (0,)), ((), ())), preferred_element_type=f32)


def against(a, b):
    return lax.dot_general(a, b, (((1,), (1,)), ((), ())), preferred_element_type=f32)


def ranks_of(mig_ref, count):
    targets = [mig_ref[0, r] for r in range(count)]
    ranks = []
    for r in range(count):
        rank = jnp.int32(0)
        for e in range(r):
            rank = rank + (targets[e] == targets[r]).astype(i32)
        ranks.append(jnp.minimum(rank, 1))
    return targets, ranks


def pack_body(rows, mig_ref, query_ref, out_ref):
    targets, ranks = ranks_of(mig_ref, rows)
    width = query_ref.shape[1]
    sub, lane = iota((rows, LANES), 0), iota((rows, LANES), 1)
    about = jnp.full((rows, LANES), -1, i32)
    for r in range(rows):
        slot = jnp.where(targets[r] >= 0, targets[r] * rows + mig_ref[1, r], -1)
        about = jnp.where((sub == r) & (lane == 0), slot, about)
        about = jnp.where((sub == r) & (lane == 1), ranks[r], about)
    about = about.astype(f32).astype(bf16)
    for d in range(out_ref.shape[0]):
        out_ref[d, :, 0:width] = query_ref[...]
        out_ref[d, :, width : width + LANES] = about


def own_body(
    rows, pages, page_len, side, pt_ref, len_ref, mig_ref, me_ref, pool, kv_ref, *refs,
):
    across, down, (whole, held, in_sem, across_sem, down_sem, whole_sem) = (
        refs[:side],
        refs[side : 2 * side],
        refs[2 * side :],
    )
    targets, ranks = ranks_of(mig_ref, rows)
    history = pages * page_len
    half = history // 2
    my_z, my_x = me_ref[0] // side, me_ref[0] % side

    def fetching(r, p):
        return pltpu.make_async_copy(
            pool.at[pt_ref[p, r]], held.at[r, pl.ds(p * page_len, page_len)], in_sem.at[r, p]
        )

    def send(r):
        to_z, to_x = targets[r] // side, targets[r] % side
        shift_x, shift_z = (to_x - my_x) & (side - 1), (to_z - my_z) & (side - 1)
        live = targets[r] >= 0
        for n in range(side):

            @pl.when(live & (shift_x == n))
            def _():
                pltpu.make_async_copy(
                    held.at[r, pl.ds(0, half)], across[n].at[to_z * 2 + ranks[r]], across_sem.at[r]
                ).start()

            @pl.when(live & (shift_z == n))
            def _():
                pltpu.make_async_copy(
                    held.at[r, pl.ds(half, half)], down[n].at[to_x * 2 + ranks[r]], down_sem.at[r]
                ).start()

    for r in range(rows):
        for p in range(pages):
            fetching(r, p).start()
    for r in range(rows):
        for p in range(pages):
            fetching(r, p).wait()
        length = len_ref[r]
        base = pl.multiple_of((length // 16) * 16, 16)
        block = held[r, pl.ds(base, 16), :].astype(f32)
        token = kv_ref[r : r + 1, :].astype(f32)
        here = iota(block.shape, 0) == length - base
        held[r, pl.ds(base, 16), :] = jnp.where(here, token, block).astype(bf16)

        send(r)
        pltpu.make_async_copy(held.at[r], whole.at[r], whole_sem.at[r]).start()

    for r in range(rows):
        pltpu.make_async_copy(held.at[r], whole.at[r], whole_sem.at[r]).wait()
    for r in range(rows):

        @pl.when(targets[r] >= 0)
        def _():
            pltpu.make_async_copy(
                held.at[r, pl.ds(0, half)], across[0].at[0], across_sem.at[r]
            ).wait()
            pltpu.make_async_copy(
                held.at[r, pl.ds(half, half)], down[0].at[0], down_sem.at[r]
            ).wait()


def self_body(rows, scale, len_ref, query_ref, whole_ref, att_ref, split_ref):
    _, history, both = whole_ref.shape
    head = both // 2
    heads = query_ref.shape[1] // head
    for h in range(heads):
        split_ref[pl.ds(h, rows, stride=heads), :] = query_ref[:, h * head : (h + 1) * head].astype(
            f32
        )
    for r in range(rows):
        queries = split_ref[r * heads : (r + 1) * heads, :].astype(bf16)
        scores = against(queries, whole_ref[r, :, 0:head]) * scale
        scores = jnp.where(iota((heads, history), 1) <= len_ref[r], scores, very_low)
        weights = jnp.exp(scores - jnp.max(scores, axis=1, keepdims=True))
        total = jnp.sum(weights, axis=1, keepdims=True)
        blended = jnp.dot(weights.astype(bf16), whole_ref[r, :, head:], preferred_element_type=f32)
        att_ref[r * heads : (r + 1) * heads, :] = (blended / total).astype(bf16)


def cross_body(
    rows, scale, mig_ref, asked_ref, image_row_ref, cache_ref, att_ref, stream_ref, out_ref,
    sorted_ref, part_ref, split_ref,
):
    images, _, both = cache_ref.shape
    head = both // 2
    everyone = asked_ref.shape[0]
    width = asked_ref.shape[1] - LANES
    heads = width // head
    group = everyone // images
    square = (everyone, everyone)
    image_row = image_row_ref[...]
    diagonal = iota(square, 1) == iota(square, 0)
    image_col = jnp.sum(
        jnp.where(diagonal, image_row.astype(f32), 0.0), axis=1, keepdims=True
    ).astype(i32)
    same = (image_col == image_row) & (iota(square, 1) < iota(square, 0))
    rank = jnp.sum(jnp.where(same, 1.0, 0.0), axis=1, keepdims=True).astype(i32)
    by_image = (iota(square, 1) == image_col * group + rank).astype(f32).astype(bf16)
    slot = asked_ref[:, width : width + 1].astype(f32).astype(i32)
    by_slot = (iota(square, 1) == slot).astype(f32).astype(bf16)
    sorted_ref[...] = onto(by_image, asked_ref[:, 0:width]).astype(bf16)
    order = onto(by_slot, by_image).astype(bf16)
    stacked = heads * group
    lane = iota((stacked, LANES), 1)
    head_of = iota((stacked, LANES), 0) // group
    for i in range(images):
        at = slice(i * group, (i + 1) * group)
        queries = jnp.concatenate(
            [sorted_ref[at, h * head : (h + 1) * head] for h in range(heads)], axis=0
        )
        scores = against(queries, cache_ref[i, :, 0:head]) * scale
        top = jnp.max(scores, axis=1, keepdims=True)
        top_hi = top.astype(bf16).astype(f32)
        top_lo = (top - top_hi).astype(bf16).astype(f32)
        weights = jnp.exp(scores - (top_hi + top_lo))
        total = jnp.sum(weights, axis=1, keepdims=True)
        total_hi = total.astype(bf16).astype(f32)
        total_lo = (total - total_hi).astype(bf16).astype(f32)
        blended = jnp.dot(weights.astype(bf16), cache_ref[i, :, head:], preferred_element_type=f32)
        blended = (blended / total).astype(bf16)
        about = jnp.zeros((stacked, LANES), f32)
        for n, stat in enumerate((top_hi, top_lo, total_hi, total_lo)):
            about = jnp.where(lane == n * heads + head_of, stat, about)
        packed = about[0:group]
        for h in range(1, heads):
            packed = packed + about[h * group : (h + 1) * group]
        for h in range(heads):
            part_ref[at, h * head : (h + 1) * head] = blended[h * group : (h + 1) * group]
        part_ref[at, width : width + LANES] = packed.astype(bf16)
    out_ref[:, 0 : width + LANES] = jnp.dot(
        order, part_ref[...], preferred_element_type=f32
    ).astype(bf16)
    targets, ranks = ranks_of(mig_ref, rows)
    chunks = stream_ref.shape[1] // LANES
    for c in range(chunks):
        split_ref[pl.ds(c, rows, stride=chunks), :] = stream_ref[
            :, c * LANES : (c + 1) * LANES
        ].astype(f32)
    lane_a = iota((1, rows * heads), 1)
    lane_s = iota((1, rows * chunks), 1)
    to_a = jnp.full(lane_a.shape, -1, i32)
    to_s = jnp.full(lane_s.shape, -1, i32)
    for r in range(rows):
        live = targets[r] >= 0
        base_a = jnp.where(live, targets[r] * rows + ranks[r] * heads, -rows * 64)
        base_s = jnp.where(live, targets[r] * rows + ranks[r] * chunks, -rows * 64)
        to_a = jnp.where(lane_a // heads == r, base_a + lane_a % heads, to_a)
        to_s = jnp.where(lane_s // chunks == r, base_s + lane_s % chunks, to_s)
    pick_a = (iota((everyone, rows * heads), 0) == to_a).astype(f32).astype(bf16)
    pick_s = (iota((everyone, rows * chunks), 0) == to_s).astype(f32).astype(bf16)
    at = width + LANES
    out_ref[:, at : at + LANES] = jnp.dot(
        pick_a, att_ref[...], preferred_element_type=f32
    ).astype(bf16)
    out_ref[:, at + LANES : at + 2 * LANES] = jnp.dot(
        pick_s, split_ref[...].astype(bf16), preferred_element_type=f32
    ).astype(bf16)


def settle_body(
    rows, me_ref, asked_ref, came_ref, att_ref, cross_ref, stream_ref, source_ref, coef_ref
):
    sources = came_ref.shape[0]
    everyone = asked_ref.shape[0]
    width = asked_ref.shape[1] - LANES
    heads = width // LANES
    chunks = stream_ref.shape[1] // LANES
    tall = (everyone, LANES)
    slot = asked_ref[:, width : width + 1].astype(f32).astype(i32)
    rank = asked_ref[:, width + 1 : width + 2].astype(f32).astype(i32)
    lane = iota(tall, 1)
    source = iota(tall, 0) // rows
    match = ((slot - me_ref[0] * rows == lane) & (lane < rows)).astype(f32).astype(bf16)
    facts = jnp.where(lane == 0, source * 2 + rank, 0)
    facts = jnp.where(lane == 1, source * rows + rank * heads, facts)
    facts = jnp.where(lane == 2, source * rows + rank * chunks, facts)
    facts = jnp.where(lane == 3, 1, facts).astype(f32).astype(bf16)
    by_lane = onto(facts, match)
    source_ref[...] = jnp.where(by_lane[3:4] > 0.5, by_lane[0:1], -1.0).astype(i32) + jnp.zeros(
        source_ref.shape, i32
    )
    by_row = onto(match, facts)[0:rows]
    live = by_row[:, 3:4] > 0.5
    base_a = jnp.where(live, by_row[:, 1:2], -4096.0).astype(i32)
    base_s = jnp.where(live, by_row[:, 2:3], -4096.0).astype(i32)
    column = iota((rows, everyone), 1)
    at = width + LANES
    own_a = came_ref[:, :, at : at + LANES].reshape(everyone, LANES)
    own_s = came_ref[:, :, at + LANES : at + 2 * LANES].reshape(everyone, LANES)
    for h in range(heads):
        pick = (column == base_a + h).astype(f32).astype(bf16)
        att_ref[:, h * LANES : (h + 1) * LANES] = jnp.dot(
            pick, own_a, preferred_element_type=f32
        ).astype(bf16)
    for c in range(chunks):
        pick = (column == base_s + c).astype(f32).astype(bf16)
        stream_ref[:, c * LANES : (c + 1) * LANES] = jnp.dot(
            pick, own_s, preferred_element_type=f32
        ).astype(bf16)
    highest = None
    for s in range(sources):
        about = came_ref[s, :, width : width + LANES].astype(f32)
        about = about + pltpu.roll(about, LANES - heads, 1)
        coef_ref[s] = about
        highest = about if s == 0 else jnp.maximum(highest, about)
    total = jnp.zeros((rows, LANES), f32)
    for s in range(sources):
        about = coef_ref[s]
        share = jnp.exp(about - highest) * pltpu.roll(about, LANES - 2 * heads, 1)
        coef_ref[s] = share
        total = total + share
    over = jnp.where(live, 1.0 / total, 0.0)
    for h in range(heads):
        blended = jnp.zeros((rows, LANES), f32)
        for s in range(sources):
            part = came_ref[s, :, h * LANES : (h + 1) * LANES].astype(f32)
            blended = blended + coef_ref[s][:, h : h + 1] * part
        blended = jnp.where(live, blended * over[:, h : h + 1], 0.0)
        cross_ref[:, h * LANES : (h + 1) * LANES] = blended.astype(bf16)


def project_body(me_ref, att_ref, cross_ref, self_w_ref, cross_w_ref, out_ref):
    rows = att_ref.shape[0]
    out_ref[0, 0:rows] = jnp.dot(att_ref[...], self_w_ref[...], preferred_element_type=f32)
    out_ref[0, rows : 2 * rows] = jnp.dot(
        cross_ref[...], cross_w_ref[...], preferred_element_type=f32
    )


def mix_body(side, me_ref, *refs):
    sent_x, sent_z = refs[:side], refs[side : 2 * side]
    next_z, next_x = refs[2 * side : 3 * side - 1], refs[3 * side - 1 : 4 * side - 2]
    held, in_sem, out_sem = refs[4 * side - 2 :]
    mine = me_ref[0] // side, me_ref[0] % side
    moves = []
    for here, came, onward in ((mine[0], sent_x, next_z), (mine[1], sent_z, next_x)):
        for shift in range(1, side):
            for n in range(side):
                at = ((here + shift) & (side - 1)) * 2
                moves.append((came[n].at[pl.ds(at, 2)], onward[shift - 1].at[pl.ds(2 * n, 2)]))
    for n, (source, _) in enumerate(moves):
        pltpu.make_async_copy(source, held.at[n], in_sem.at[n]).start()
    for n, (source, target) in enumerate(moves):
        pltpu.make_async_copy(source, held.at[n], in_sem.at[n]).wait()
        pltpu.make_async_copy(held.at[n], target, out_sem.at[n]).start()
    for n, (_, target) in enumerate(moves):
        pltpu.make_async_copy(held.at[n], target, out_sem.at[n]).wait()


def place_body(side, source_ref, me_ref, *refs):
    near_x, far_z = refs[:side], refs[side : 2 * side - 1]
    near_z, far_x = refs[2 * side - 1 : 3 * side - 1], refs[3 * side - 1 : 4 * side - 2]
    out, held, first_sem, last_sem, out_sem = refs[4 * side - 2 :]
    rows, history, _ = held.shape
    half = history // 2
    my_z, my_x = me_ref[0] // side, me_ref[0] % side

    def fetch(ref, at, t, begin, sem):
        return pltpu.make_async_copy(ref.at[at], held.at[t, pl.ds(begin, half)], sem.at[t])

    def begin(t, carry):
        code = source_ref[0, t]
        live = code >= 0
        code = jnp.maximum(code, 0)
        source, rank = code // 2, code % 2
        shift_z = (my_z - source // side) & (side - 1)
        shift_x = (my_x - source % side) & (side - 1)
        for n in range(side):

            @pl.when(live & (shift_z == 0) & (shift_x == n))
            def _():
                fetch(near_x[n], my_z * 2 + rank, t, 0, first_sem).start()

            @pl.when(live & (shift_x == 0) & (shift_z == n))
            def _():
                fetch(near_z[n], my_x * 2 + rank, t, half, last_sem).start()

        for n in range(1, side):

            @pl.when(live & (shift_z == n))
            def _():
                fetch(far_z[n - 1], shift_x * 2 + rank, t, 0, first_sem).start()

            @pl.when(live & (shift_x == n))
            def _():
                fetch(far_x[n - 1], shift_z * 2 + rank, t, half, last_sem).start()

        @pl.when(jnp.logical_not(live))
        def _():
            held[t] = jnp.zeros(held.shape[1:], bf16)

        return carry

    def finish(t, carry):
        @pl.when(source_ref[0, t] >= 0)
        def _():
            fetch(near_x[0], 0, t, 0, first_sem).wait()
            fetch(near_z[0], 0, t, half, last_sem).wait()

        pltpu.make_async_copy(held.at[t], out.at[t], out_sem.at[t]).start()
        return carry

    lax.fori_loop(0, rows, begin, 0)
    lax.fori_loop(0, rows, finish, 0)
    for t in range(rows):
        pltpu.make_async_copy(held.at[t], out.at[t], out_sem.at[t]).wait()


def in_order(found, shifts):
    return [found[0]] + [found[1 + shifts.index(n)] for n in range(1, len(found))]


def per_device(
    stream,
    self_query,
    new_kv,
    cache_pool,
    page_table,
    lengths,
    migration,
    image_of,
    cross_query,
    image_cache,
    self_output,
    cross_output,
    cross_gate,
):
    rows, width = cross_query.shape
    devices = lax.axis_size("rows")
    columns = lax.axis_size("heads")
    everyone = rows * devices
    pages = page_table.shape[1]
    pool_pages, page_len, _, both = cache_pool.shape
    head = both // 2
    heads = width // head
    history = pages * page_len
    images, tokens = image_cache.shape[:2]
    part = stream.shape[1]
    chunks = part // LANES
    scale = 1.0 / math.sqrt(head)
    out_width = self_output.shape[1]
    shape = jax.ShapeDtypeStruct
    mig = migration.T
    my_row = lax.axis_index("rows").astype(i32)[None]
    my_column = lax.axis_index("heads").astype(i32)[None]

    packed = pl.pallas_call(
        functools.partial(pack_body, rows),
        out_shape=shape((devices, rows, width + LANES), bf16),
        in_specs=[smem(), vmem()],
        out_specs=vmem(),
        name="pack",
    )(mig, cross_query)
    asked = lax.all_to_all(packed, "rows", 0, 0, tiled=True).reshape(everyone, width + LANES)

    side = math.isqrt(devices)
    shifts = (1, *range(side - 1, 1, -1))
    half = history // 2
    bucket = shape((2 * side, half, both), bf16)
    *buckets, whole = pl.pallas_call(
        functools.partial(own_body, rows, pages, page_len, side),
        out_shape=(*([bucket] * (2 * side)), shape((rows, history, both), bf16)),
        in_specs=[smem(), smem(), smem(), smem(), anywhere(), vmem()],
        out_specs=(*([anywhere()] * (2 * side)), anywhere()),
        scratch_shapes=[
            VMEM((rows, history, both), bf16),
            pltpu.SemaphoreType.DMA((rows, pages)),
            pltpu.SemaphoreType.DMA((rows,)),
            pltpu.SemaphoreType.DMA((rows,)),
            pltpu.SemaphoreType.DMA((rows,)),
        ],
        compiler_params=pltpu.CompilerParams(vmem_limit_bytes=61 << 20),
        cost_estimate=pl.CostEstimate(
            flops=0, bytes_accessed=6 * rows * history * both, transcendentals=0
        ),
        name="own",
    )(
        page_table.T,
        lengths,
        mig,
        my_row,
        cache_pool.reshape(pool_pages, page_len, both),
        new_kv.reshape(rows, both),
    )
    attended = pl.pallas_call(
        functools.partial(self_body, rows, scale),
        out_shape=shape((rows * heads, head), bf16),
        in_specs=[smem(), vmem(), vmem()],
        out_specs=vmem(),
        scratch_shapes=[VMEM((rows * heads, head), f32)],
        cost_estimate=pl.CostEstimate(
            flops=4 * rows * heads * history * head,
            bytes_accessed=2 * rows * history * both,
            transcendentals=rows * heads * history,
        ),
        name="attend",
    )(lengths, self_query, whole)

    def along(dz, dx):
        return [
            (z * side + x, ((z + dz) % side) * side + (x + dx) % side)
            for z in range(side)
            for x in range(side)
        ]

    near_x, near_z = [buckets[0]], [buckets[side]]
    for n in shifts:
        near_x.append(lax.ppermute(buckets[n], "rows", along(0, n)))
        near_z.append(lax.ppermute(buckets[side + n], "rows", along(n, 0)))
    near_x, near_z = in_order(near_x, shifts), in_order(near_z, shifts)

    message_width = width + 3 * LANES
    message = pl.pallas_call(
        functools.partial(cross_body, rows, scale),
        out_shape=shape((everyone, message_width), bf16),
        in_specs=[smem(), vmem(), vmem(), vmem(), vmem(), vmem()],
        out_specs=vmem(),
        scratch_shapes=[
            VMEM((everyone, width), bf16),
            VMEM((everyone, width + LANES), bf16),
            VMEM((rows * chunks, LANES), f32),
        ],
        cost_estimate=pl.CostEstimate(
            flops=4 * everyone * heads * tokens * head + 8 * everyone * everyone * width,
            bytes_accessed=2 * images * tokens * both + 4 * everyone * width,
            transcendentals=everyone * heads * tokens,
        ),
        compiler_params=pltpu.CompilerParams(vmem_limit_bytes=40 << 20),
        name="cross",
    )(
        mig,
        asked,
        image_of.reshape(1, everyone),
        image_cache.reshape(images, tokens, both),
        attended,
        stream,
    )
    came = lax.all_to_all(message.reshape(devices, rows, message_width), "rows", 0, 0, tiled=True)
    onward = pl.pallas_call(
        functools.partial(mix_body, side),
        out_shape=[bucket] * (2 * side - 2),
        in_specs=[smem()] + [anywhere()] * (2 * side),
        out_specs=[anywhere()] * (2 * side - 2),
        scratch_shapes=[
            VMEM((2 * side * (side - 1), 2, half, both), bf16),
            pltpu.SemaphoreType.DMA((2 * side * (side - 1),)),
            pltpu.SemaphoreType.DMA((2 * side * (side - 1),)),
        ],
        cost_estimate=pl.CostEstimate(
            flops=0, bytes_accessed=8 * rows * history * both, transcendentals=0
        ),
        name="mix",
    )(my_row, *near_x, *near_z)
    far_z, far_x = [None], [None]
    for n in shifts:
        far_z.append(lax.ppermute(onward[n - 1], "rows", along(n, 0)))
        far_x.append(lax.ppermute(onward[side - 1 + n - 1], "rows", along(0, n)))
    far_z, far_x = in_order(far_z, shifts)[1:], in_order(far_x, shifts)[1:]

    slot_attended, slot_cross, slot_stream, source = pl.pallas_call(
        functools.partial(settle_body, rows),
        out_shape=(
            shape((rows, width), bf16),
            shape((rows, width), bf16),
            shape((rows, part), bf16),
            shape((8, LANES), i32),
        ),
        in_specs=[smem(), vmem(), vmem()],
        out_specs=(vmem(), vmem(), vmem(), vmem()),
        scratch_shapes=[VMEM((devices, rows, LANES), f32)],
        cost_estimate=pl.CostEstimate(
            flops=4 * everyone * width,
            bytes_accessed=4 * everyone * width,
            transcendentals=everyone * LANES,
        ),
        compiler_params=pltpu.CompilerParams(vmem_limit_bytes=61 << 20),
        name="combine",
    )(my_row, asked, came)

    parts = pl.pallas_call(
        project_body,
        grid_spec=pltpu.PrefetchScalarGridSpec(
            num_scalar_prefetch=1,
            grid=(columns,),
            in_specs=[
                pl.BlockSpec((rows, width), lambda o, me: (0, 0)),
                pl.BlockSpec((rows, width), lambda o, me: (0, 0)),
                pl.BlockSpec((width, part), lambda o, me: (0, lax.rem(me[0] + o, columns))),
                pl.BlockSpec((width, part), lambda o, me: (0, lax.rem(me[0] + o, columns))),
            ],
            out_specs=pl.BlockSpec((1, 2 * rows, part), lambda o, me: (o, 0, 0)),
        ),
        out_shape=shape((columns, 2 * rows, part), f32),
        cost_estimate=pl.CostEstimate(
            flops=4 * rows * width * out_width,
            bytes_accessed=4 * width * out_width,
            transcendentals=0,
        ),
        compiler_params=pltpu.CompilerParams(vmem_limit_bytes=61 << 20),
        name="project",
    )(my_column, slot_attended, slot_cross, self_output, cross_output)
    summed = parts[0]
    for o in range(1, columns):
        summed = summed + lax.ppermute(
            parts[o], "heads", [(c, (c + o) % columns) for c in range(columns)]
        )
    self_update = (slot_stream.astype(f32) + summed[:rows]).astype(bf16)
    cross_update = (jnp.tanh(cross_gate[0]) * summed[rows:]).astype(bf16)

    new_cache = pl.pallas_call(
        functools.partial(place_body, side),
        in_specs=[smem(), smem()] + [anywhere()] * (4 * side - 2),
        out_specs=anywhere(),
        out_shape=shape((rows, history, both), bf16),
        scratch_shapes=[
            VMEM((rows, history, both), bf16),
            pltpu.SemaphoreType.DMA((rows,)),
            pltpu.SemaphoreType.DMA((rows,)),
            pltpu.SemaphoreType.DMA((rows,)),
        ],
        cost_estimate=pl.CostEstimate(
            flops=0, bytes_accessed=4 * rows * history * both, transcendentals=0
        ),
        name="place",
    )(source, my_row, *near_x, *far_z, *near_z, *far_x)
    return (self_update, cross_update, new_cache.reshape(rows, history, 1, both))


def solution(mesh):
    in_specs = (
        P("rows", "heads"),
        P("rows", "heads"),
        P("rows", "heads", None),
        P("rows", None, "heads", None),
        P("rows", None),
        P("rows"),
        P("rows", None),
        P(),
        P("rows", "heads"),
        P(None, "rows", "heads", None),
        P("heads", None),
        P("heads", None),
        P(),
    )
    out_specs = (P("rows", "heads"), P("rows", "heads"), P("rows", None, "heads", None))

    return jax.shard_map(
        per_device, mesh=mesh, in_specs=in_specs, out_specs=out_specs, check_vma=False
    )
```

profile of v0, /device:TPU:0, one launch (start us, length us, event | category | flops | bytes accessed | tf_op | source)
XLA Modules:
  0.0 147.4 jit_solution(1493882591230212993)
XLA Ops:
  0.6 5.7 %own.1 = (bf16[8,192,256]{2,1,0:T(8,128)(2,1)}, bf16[8,192,256]{2,1,0:T(8,128)(2,1)}, bf16[8,192,256]{2,1,0:T(8,128)(2,1)}, bf16[8,192,256]{2,1,0:T(8,128)(2,1)}...) custom-call(s32[6,16]{1,0:T(8,128)} %bitcast.54, ...), custom_call_target="tpu_custom_call" | custom-call | bytes 9437184 | tf_op jit(solution)/shard_map/own/pallas_call | solution.py:434
  7.8 1.8 %pack.1 = bf16[16,16,1152]{2,1,0:T(8,128)(2,1)} custom-call(s32[2,16]{1,0:T(2,128)} %bitcast.47, bf16[16,1024]{1,0:T(8,128)(2,1)} %query_ref.2), custom_call_target="tpu_custom_call" | custom-call | tf_op jit(solution)/shard_map/pack/pallas_call | solution.py:421
  9.6 7.7 %all-to-all-start = ((bf16[16,16,1152]{2,1,0:T(8,128)(2,1)}), bf16[16,16,1152]{2,1,0:T(8,128)(2,1)S(1)}, u32[]{:S(2)}, u32[]{:S(2)}) async-start(bf16[16,16,1152]{2,1,0:T(8,128)(2,1)} %pack.1), calls=%async_computation | async-start | bytes 1179648 | tf_op jit(solution)/shard_map/all_to_all | solution.py:428
  17.3 3.4 %collective-permute-start.8 = (bf16[8,192,256]{2,1,0:T(8,128)(2,1)}, bf16[8,192,256]{2,1,0:T(8,128)(2,1)}, u32[]{:S(2)}, u32[]{:S(2)}) collective-permute-start(bf16[8,192,256]{2,1,0:T(8,128)(2,1)} %get-tuple-element.29), channel_id=1, source_target_pairs={{0,16},{8,24},{16,0},{24,8},{32,48},{40,56},{48,32},{56,40},{64,80... | collective-permute-start | bytes 2359304 | tf_op jit(solution)/shard_map/ppermute | solution.py:482
  23.4 2.7 %collective-permute-start.11 = (bf16[8,192,256]{2,1,0:T(8,128)(2,1)}, bf16[8,192,256]{2,1,0:T(8,128)(2,1)}, u32[]{:S(2)}, u32[]{:S(2)}) collective-permute-start(bf16[8,192,256]{2,1,0:T(8,128)(2,1)} %get-tuple-element.33), channel_id=1, source_target_pairs={{0,64},{8,72},{16,80},{24,88},{32,96},{40,104},{48,112},{56,120},{... | collective-permute-start | bytes 2359304 | tf_op jit(solution)/shard_map/ppermute | solution.py:483
  26.0 3.6 %collective-permute-done.7.refs_1_ = bf16[8,192,256]{2,1,0:T(8,128)(2,1)S(1)} collective-permute-done((bf16[8,192,256]{2,1,0:T(8,128)(2,1)}, bf16[8,192,256]{2,1,0:T(8,128)(2,1)S(1)}, u32[]{:S(2)}, u32[]{:S(2)}) %collective-permute-start.7) | collective-permute-done | bytes 786464 | tf_op jit(solution)/shard_map/ppermute | solution.py:482
  29.7 4.4 %collective-permute-start.12 = (bf16[8,192,256]{2,1,0:T(8,128)(2,1)}, bf16[8,192,256]{2,1,0:T(8,128)(2,1)}, u32[]{:S(2)}, u32[]{:S(2)}) collective-permute-start(bf16[8,192,256]{2,1,0:T(8,128)(2,1)} %get-tuple-element.34), channel_id=1, source_target_pairs={{0,96},{8,104},{16,112},{24,120},{32,0},{40,8},{48,16},{56,24},{64... | collective-permute-start | bytes 2359304 | tf_op jit(solution)/shard_map/ppermute | solution.py:483
  34.0 6.4 %attend.1.att_ref = bf16[128,128]{1,0:T(8,128)(2,1)} custom-call(s32[16]{0:T(128)} %len_ref.3, bf16[16,1024]{1,0:T(8,128)(2,1)} %query_ref.3, bf16[16,384,256]{2,1,0:T(8,128)(2,1)} %get-tuple-element.22.whole_ref), custom_call_target="tpu_custom_call" | custom-call | flops 25165824 | bytes 3145728 | tf_op jit(solution)/shard_map/attend/pallas_call | solution.py:459
  41.3 6.2 %cross.1 = bf16[256,1408]{1,0:T(8,128)(2,1)} custom-call(s32[2,16]{1,0:T(2,128)S(1)} %bitcast.48, bf16[256,1152]{1,0:T(8,128)(2,1)S(1)} %bitcast.44, s32[1,256]{1,0:T(1,128)S(1)} %bitcast.50, bf16[16,128,256]{2,1,0:T(8,128)(2,1)S(1)} %bitcast.49, bf16[128,128]{1,0:T(8,128)(2,1)S(1)} %copy-done.1, bf16[16,512]{1,0:T(8,128)(2,1)S(1)} %copy-done.4), custom_call_target="tpu_custom_call" | custom-call | flops 671088640 | bytes 2097152 | tf_op jit(solution)/shard_map/cross/pallas_call | solution.py:487
  47.5 19.0 %all-to-all-start.1 = ((bf16[16,16,1408]{2,1,0:T(8,128)(2,1)}), bf16[16,16,1408]{2,1,0:T(8,128)(2,1)S(1)}, u32[]{:S(2)}, u32[]{:S(2)}) async-start(bf16[16,16,1408]{2,1,0:T(8,128)(2,1)} %bitcast.8), calls=%async_computation.1 | async-start | bytes 1441792 | tf_op jit(solution)/shard_map/all_to_all | solution.py:512
  67.0 4.8 %mix.1 = (bf16[8,192,256]{2,1,0:T(8,128)(2,1)}, bf16[8,192,256]{2,1,0:T(8,128)(2,1)}, bf16[8,192,256]{2,1,0:T(8,128)(2,1)}, bf16[8,192,256]{2,1,0:T(8,128)(2,1)}...) custom-call(s32[1]{0:T(128)} %bitcast.me_ref, bf16[8,192,256]{2,1,0:T(8,128)(2,1)} %get-tuple-element.27.refs_0_, ...), custom_call_target="tpu_custom_call" | custom-call | bytes 12582912 | tf_op jit(solution)/shard_map/mix/pallas_call | solution.py:513
  71.8 1.6 %collective-permute-start.13 = (bf16[8,192,256]{2,1,0:T(8,128)(2,1)}, bf16[8,192,256]{2,1,0:T(8,128)(2,1)S(1)}, u32[]{:S(2)}, u32[]{:S(2)}) collective-permute-start(bf16[8,192,256]{2,1,0:T(8,128)(2,1)} %get-tuple-element.35), channel_id=1, source_target_pairs={{0,32},{8,40},{16,48},{24,56},{32,64},{40,72},{48,80},{56,88},{64,... | collective-permute-start | bytes 2359304 | tf_op jit(solution)/shard_map/ppermute | solution.py:530
  73.4 4.3 %all-to-all-done.1.came_ref = bf16[16,16,1408]{2,1,0:T(8,128)(2,1)S(1)} async-done(((bf16[16,16,1408]{2,1,0:T(8,128)(2,1)}), bf16[16,16,1408]{2,1,0:T(8,128)(2,1)S(1)}, u32[]{:S(2)}, u32[]{:S(2)}) %all-to-all-start.1) | async-done | bytes 720928 | tf_op jit(solution)/shard_map/all_to_all | solution.py:512
  78.6 2.8 %combine.1 = (bf16[16,1024]{1,0:T(8,128)(2,1)}, bf16[16,1024]{1,0:T(8,128)(2,1)}, bf16[16,512]{1,0:T(8,128)(2,1)}, s32[8,128]{1,0:T(8,128)}) custom-call(s32[1]{0:T(128)} %bitcast.me_ref, bf16[256,1152]{1,0:T(8,128)(2,1)} %bitcast.45, bf16[16,16,1408]{2,1,0:T(8,128)(2,1)} %copy-done.7), custom_call_target="tpu_custom_call" | custom-call | flops 1048576 | bytes 1048576 | tf_op jit(solution)/shard_map/combine/pallas_call | solution.py:534
  81.3 9.6 %project.1 = f32[8,32,512]{2,1,0:T(8,128)} custom-call(s32[1]{0:T(128)} %bitcast.9.me_ref, bf16[16,1024]{1,0:T(8,128)(2,1)} %get-tuple-element.24.att_ref, bf16[16,1024]{1,0:T(8,128)(2,1)} %get-tuple-element.25.cross_ref, bf16[1024,4096]{1,0:T(8,128)(2,1)} %self_w_ref.1, bf16[1024,4096]{1,0:T(8,128)(2,1)} %cross_w_ref.1), custom_call_target="tpu_custom_call" | custom-call | flops 268435456 | bytes 16777216 | tf_op jit(solution)/shard_map/project/pallas_call | solution.py:554
  92.0 2.9 %collective-permute-start.6 = (f32[32,512]{1,0:T(8,128)S(1)}, f32[32,512]{1,0:T(8,128)S(1)}, u32[]{:S(2)}, u32[]{:S(2)}) collective-permute-start(f32[32,512]{1,0:T(8,128)S(1)} %get-tuple-element.45), channel_id=1, source_target_pairs={{0,7},{1,0},{2,1},{3,2},{4,3},{5,4},{6,5},{7,6},{8,15},{9,8},{10,9... | collective-permute-start | bytes 196616 | tf_op jit(solution)/shard_map/ppermute | solution.py:578
  95.0 1.8 %collective-permute-start.5 = (f32[32,512]{1,0:T(8,128)S(1)}, f32[32,512]{1,0:T(8,128)S(1)}, u32[]{:S(2)}, u32[]{:S(2)}) collective-permute-start(f32[32,512]{1,0:T(8,128)S(1)} %get-tuple-element.46), channel_id=1, source_target_pairs={{0,6},{1,7},{2,0},{3,1},{4,2},{5,3},{6,4},{7,5},{8,14},{9,15},{10,... | collective-permute-start | bytes 196616 | tf_op jit(solution)/shard_map/ppermute | solution.py:578
  96.9 2.0 %collective-permute-start.3 = (f32[32,512]{1,0:T(8,128)S(1)}, f32[32,512]{1,0:T(8,128)S(1)}, u32[]{:S(2)}, u32[]{:S(2)}) collective-permute-start(f32[32,512]{1,0:T(8,128)S(1)} %get-tuple-element.48), channel_id=1, source_target_pairs={{0,4},{1,5},{2,6},{3,7},{4,0},{5,1},{6,2},{7,3},{8,12},{9,13},{10,... | collective-permute-start | bytes 196616 | tf_op jit(solution)/shard_map/ppermute | solution.py:578
  104.9 2.9 %collective-permute-done.1 = f32[32,512]{1,0:T(8,128)S(1)} collective-permute-done((f32[32,512]{1,0:T(8,128)S(1)}, f32[32,512]{1,0:T(8,128)S(1)}, u32[]{:S(2)}, u32[]{:S(2)}) %collective-permute-start.1) | collective-permute-done | bytes 65568 | tf_op jit(solution)/shard_map/ppermute | solution.py:578
  108.8 2.4 %collective-permute-start.18 = (bf16[8,192,256]{2,1,0:T(8,128)(2,1)}, bf16[8,192,256]{2,1,0:T(8,128)(2,1)}, u32[]{:S(2)}, u32[]{:S(2)}) collective-permute-start(bf16[8,192,256]{2,1,0:T(8,128)(2,1)} %get-tuple-element.40), channel_id=1, source_target_pairs={{0,24},{8,0},{16,8},{24,16},{32,56},{40,32},{48,40},{56,48},{64,88... | collective-permute-start | bytes 2359304 | tf_op jit(solution)/shard_map/ppermute | solution.py:531
  113.4 8.8 %collective-permute-done.14.refs_5_ = bf16[8,192,256]{2,1,0:T(8,128)(2,1)S(1)} collective-permute-done((bf16[8,192,256]{2,1,0:T(8,128)(2,1)}, bf16[8,192,256]{2,1,0:T(8,128)(2,1)S(1)}, u32[]{:S(2)}, u32[]{:S(2)}) %collective-permute-start.14) | collective-permute-done | bytes 786464 | tf_op jit(solution)/shard_map/ppermute | solution.py:530
  122.2 15.2 %collective-permute-done.15.refs_6_ = bf16[8,192,256]{2,1,0:T(8,128)(2,1)S(1)} collective-permute-done((bf16[8,192,256]{2,1,0:T(8,128)(2,1)}, bf16[8,192,256]{2,1,0:T(8,128)(2,1)S(1)}, u32[]{:S(2)}, u32[]{:S(2)}) %collective-permute-start.15) | collective-permute-done | bytes 786464 | tf_op jit(solution)/shard_map/ppermute | solution.py:530
  137.3 5.3 %collective-permute-done.16.refs_11_ = bf16[8,192,256]{2,1,0:T(8,128)(2,1)} collective-permute-done((bf16[8,192,256]{2,1,0:T(8,128)(2,1)}, bf16[8,192,256]{2,1,0:T(8,128)(2,1)}, u32[]{:S(2)}, u32[]{:S(2)}) %collective-permute-start.16) | collective-permute-done | bytes 786464 | tf_op jit(solution)/shard_map/ppermute | solution.py:531
  143.3 4.1 %place.1 = bf16[16,384,256]{2,1,0:T(8,128)(2,1)} custom-call(s32[8,128]{1,0:T(8,128)} %get-tuple-element.26.source_ref, s32[1]{0:T(128)} %bitcast.me_ref, bf16[8,192,256]{2,1,0:T(8,128)(2,1)} %get-tuple-element.27.refs_0_, bf16[8,192,256]{2,1,0:T(8,128)(2,1)} %copy-done.6, bf16[8,192,256]{2,1,0:T(8,128)(2,1)} %collective-permute-done.8.refs_2_, ...), custom_call_target="tpu_custom_call" | custom-call | bytes 6291456 | tf_op jit(solution)/shard_map/place/pallas_call | solution.py:584
  (53 shorter events, 16.4 us)
Async XLA Ops:
  6.3 34.1 %copy-start.2 = (s32[16,2]{0,1:T(2,128)S(1)}, s32[16,2]{0,1:T(2,128)}, u32[]{:S(2)}) copy-start(s32[16,2]{0,1:T(2,128)} %param.19) | copy-start | bytes 388
  6.3 34.1 %copy-start.3 = (bf16[16,128,1,256]{3,1,2,0:T(8,128)(2,1)S(1)}, bf16[16,128,1,256]{3,1,2,0:T(8,128)(2,1)}, u32[]{:S(2)}) copy-start(bf16[16,128,1,256]{3,1,2,0:T(8,128)(2,1)} %param.22) | copy-start | bytes 3145732
  6.4 23.3 %collective-permute-start.7 = (bf16[8,192,256]{2,1,0:T(8,128)(2,1)}, bf16[8,192,256]{2,1,0:T(8,128)(2,1)S(1)}, u32[]{:S(2)}, u32[]{:S(2)}) collective-permute-start(bf16[8,192,256]{2,1,0:T(8,128)(2,1)} %get-tuple-element.28), channel_id=1, source_target_pairs={{0,8},{8,16},{16,24},{24,0},{32,40},{40,48},{48,56},{56,32},{64,72... | collective-permute-start | bytes 2359304 | tf_op jit(solution)/shard_map/ppermute | solution.py:482
  9.6 30.9 %all-to-all-start = ((bf16[16,16,1152]{2,1,0:T(8,128)(2,1)}), bf16[16,16,1152]{2,1,0:T(8,128)(2,1)S(1)}, u32[]{:S(2)}, u32[]{:S(2)}) async-start(bf16[16,16,1152]{2,1,0:T(8,128)(2,1)} %pack.1), calls=%async_computation | async-start | bytes 1179648 | tf_op jit(solution)/shard_map/all_to_all | solution.py:428
  17.3 49.2 %collective-permute-start.8 = (bf16[8,192,256]{2,1,0:T(8,128)(2,1)}, bf16[8,192,256]{2,1,0:T(8,128)(2,1)}, u32[]{:S(2)}, u32[]{:S(2)}) collective-permute-start(bf16[8,192,256]{2,1,0:T(8,128)(2,1)} %get-tuple-element.29), channel_id=1, source_target_pairs={{0,16},{8,24},{16,0},{24,8},{32,48},{40,56},{48,32},{56,40},{64,80... | collective-permute-start | bytes 2359304 | tf_op jit(solution)/shard_map/ppermute | solution.py:482
  20.7 45.8 %collective-permute-start.9 = (bf16[8,192,256]{2,1,0:T(8,128)(2,1)}, bf16[8,192,256]{2,1,0:T(8,128)(2,1)}, u32[]{:S(2)}, u32[]{:S(2)}) collective-permute-start(bf16[8,192,256]{2,1,0:T(8,128)(2,1)} %get-tuple-element.30), channel_id=1, source_target_pairs={{0,24},{8,0},{16,8},{24,16},{32,56},{40,32},{48,40},{56,48},{64,88... | collective-permute-start | bytes 2359304 | tf_op jit(solution)/shard_map/ppermute | solution.py:482
  21.9 44.7 %collective-permute-start.10 = (bf16[8,192,256]{2,1,0:T(8,128)(2,1)}, bf16[8,192,256]{2,1,0:T(8,128)(2,1)}, u32[]{:S(2)}, u32[]{:S(2)}) collective-permute-start(bf16[8,192,256]{2,1,0:T(8,128)(2,1)} %get-tuple-element.32), channel_id=1, source_target_pairs={{0,32},{8,40},{16,48},{24,56},{32,64},{40,72},{48,80},{56,88},{64,... | collective-permute-start | bytes 2359304 | tf_op jit(solution)/shard_map/ppermute | solution.py:483
  23.4 43.6 %collective-permute-start.11 = (bf16[8,192,256]{2,1,0:T(8,128)(2,1)}, bf16[8,192,256]{2,1,0:T(8,128)(2,1)}, u32[]{:S(2)}, u32[]{:S(2)}) collective-permute-start(bf16[8,192,256]{2,1,0:T(8,128)(2,1)} %get-tuple-element.33), channel_id=1, source_target_pairs={{0,64},{8,72},{16,80},{24,88},{32,96},{40,104},{48,112},{56,120},{... | collective-permute-start | bytes 2359304 | tf_op jit(solution)/shard_map/ppermute | solution.py:483
  29.7 37.3 %collective-permute-start.12 = (bf16[8,192,256]{2,1,0:T(8,128)(2,1)}, bf16[8,192,256]{2,1,0:T(8,128)(2,1)}, u32[]{:S(2)}, u32[]{:S(2)}) collective-permute-start(bf16[8,192,256]{2,1,0:T(8,128)(2,1)} %get-tuple-element.34), channel_id=1, source_target_pairs={{0,96},{8,104},{16,112},{24,120},{32,0},{40,8},{48,16},{56,24},{64... | collective-permute-start | bytes 2359304 | tf_op jit(solution)/shard_map/ppermute | solution.py:483
  47.5 30.2 %all-to-all-start.1 = ((bf16[16,16,1408]{2,1,0:T(8,128)(2,1)}), bf16[16,16,1408]{2,1,0:T(8,128)(2,1)S(1)}, u32[]{:S(2)}, u32[]{:S(2)}) async-start(bf16[16,16,1408]{2,1,0:T(8,128)(2,1)} %bitcast.8), calls=%async_computation.1 | async-start | bytes 1441792 | tf_op jit(solution)/shard_map/all_to_all | solution.py:512
  71.8 37.0 %collective-permute-start.13 = (bf16[8,192,256]{2,1,0:T(8,128)(2,1)}, bf16[8,192,256]{2,1,0:T(8,128)(2,1)S(1)}, u32[]{:S(2)}, u32[]{:S(2)}) collective-permute-start(bf16[8,192,256]{2,1,0:T(8,128)(2,1)} %get-tuple-element.35), channel_id=1, source_target_pairs={{0,32},{8,40},{16,48},{24,56},{32,64},{40,72},{48,80},{56,88},{64,... | collective-permute-start | bytes 2359304 | tf_op jit(solution)/shard_map/ppermute | solution.py:530
  92.0 4.9 %collective-permute-start = (f32[32,512]{1,0:T(8,128)S(1)}, f32[32,512]{1,0:T(8,128)S(1)}, u32[]{:S(2)}, u32[]{:S(2)}) collective-permute-start(f32[32,512]{1,0:T(8,128)S(1)} %get-tuple-element.44), channel_id=1, source_target_pairs={{0,1},{1,2},{2,3},{3,4},{4,5},{5,6},{6,7},{7,0},{8,9},{9,10},{10,1... | collective-permute-start | bytes 196616 | tf_op jit(solution)/shard_map/ppermute | solution.py:578
  92.0 6.9 %collective-permute-start.6 = (f32[32,512]{1,0:T(8,128)S(1)}, f32[32,512]{1,0:T(8,128)S(1)}, u32[]{:S(2)}, u32[]{:S(2)}) collective-permute-start(f32[32,512]{1,0:T(8,128)S(1)} %get-tuple-element.45), channel_id=1, source_target_pairs={{0,7},{1,0},{2,1},{3,2},{4,3},{5,4},{6,5},{7,6},{8,15},{9,8},{10,9... | collective-permute-start | bytes 196616 | tf_op jit(solution)/shard_map/ppermute | solution.py:578
  95.0 4.7 %collective-permute-start.5 = (f32[32,512]{1,0:T(8,128)S(1)}, f32[32,512]{1,0:T(8,128)S(1)}, u32[]{:S(2)}, u32[]{:S(2)}) collective-permute-start(f32[32,512]{1,0:T(8,128)S(1)} %get-tuple-element.46), channel_id=1, source_target_pairs={{0,6},{1,7},{2,0},{3,1},{4,2},{5,3},{6,4},{7,5},{8,14},{9,15},{10,... | collective-permute-start | bytes 196616 | tf_op jit(solution)/shard_map/ppermute | solution.py:578
  96.8 3.9 %collective-permute-start.4 = (f32[32,512]{1,0:T(8,128)S(1)}, f32[32,512]{1,0:T(8,128)S(1)}, u32[]{:S(2)}, u32[]{:S(2)}) collective-permute-start(f32[32,512]{1,0:T(8,128)S(1)} %get-tuple-element.47), channel_id=1, source_target_pairs={{0,5},{1,6},{2,7},{3,0},{4,1},{5,2},{6,3},{7,4},{8,13},{9,14},{10,... | collective-permute-start | bytes 196616 | tf_op jit(solution)/shard_map/ppermute | solution.py:578
  96.9 6.2 %collective-permute-start.3 = (f32[32,512]{1,0:T(8,128)S(1)}, f32[32,512]{1,0:T(8,128)S(1)}, u32[]{:S(2)}, u32[]{:S(2)}) collective-permute-start(f32[32,512]{1,0:T(8,128)S(1)} %get-tuple-element.48), channel_id=1, source_target_pairs={{0,4},{1,5},{2,6},{3,7},{4,0},{5,1},{6,2},{7,3},{8,12},{9,13},{10,... | collective-permute-start | bytes 196616 | tf_op jit(solution)/shard_map/ppermute | solution.py:578
  98.9 5.4 %collective-permute-start.2 = (f32[32,512]{1,0:T(8,128)S(1)}, f32[32,512]{1,0:T(8,128)S(1)}, u32[]{:S(2)}, u32[]{:S(2)}) collective-permute-start(f32[32,512]{1,0:T(8,128)S(1)} %get-tuple-element.49), channel_id=1, source_target_pairs={{0,3},{1,4},{2,5},{3,6},{4,7},{5,0},{6,1},{7,2},{8,11},{9,12},{10,... | collective-permute-start | bytes 196616 | tf_op jit(solution)/shard_map/ppermute | solution.py:578
  99.7 8.2 %collective-permute-start.1 = (f32[32,512]{1,0:T(8,128)S(1)}, f32[32,512]{1,0:T(8,128)S(1)}, u32[]{:S(2)}, u32[]{:S(2)}) collective-permute-start(f32[32,512]{1,0:T(8,128)S(1)} %get-tuple-element.50), channel_id=1, source_target_pairs={{0,2},{1,3},{2,4},{3,5},{4,6},{5,7},{6,0},{7,1},{8,10},{9,11},{10,... | collective-permute-start | bytes 196616 | tf_op jit(solution)/shard_map/ppermute | solution.py:578
  100.6 21.5 %collective-permute-start.14 = (bf16[8,192,256]{2,1,0:T(8,128)(2,1)}, bf16[8,192,256]{2,1,0:T(8,128)(2,1)S(1)}, u32[]{:S(2)}, u32[]{:S(2)}) collective-permute-start(bf16[8,192,256]{2,1,0:T(8,128)(2,1)} %get-tuple-element.36), channel_id=1, source_target_pairs={{0,64},{8,72},{16,80},{24,88},{32,96},{40,104},{48,112},{56,120},{... | collective-permute-start | bytes 2359304 | tf_op jit(solution)/shard_map/ppermute | solution.py:530
  103.1 34.2 %collective-permute-start.15 = (bf16[8,192,256]{2,1,0:T(8,128)(2,1)}, bf16[8,192,256]{2,1,0:T(8,128)(2,1)S(1)}, u32[]{:S(2)}, u32[]{:S(2)}) collective-permute-start(bf16[8,192,256]{2,1,0:T(8,128)(2,1)} %get-tuple-element.37), channel_id=1, source_target_pairs={{0,96},{8,104},{16,112},{24,120},{32,0},{40,8},{48,16},{56,24},{64... | collective-permute-start | bytes 2359304 | tf_op jit(solution)/shard_map/ppermute | solution.py:530
  104.3 38.4 %collective-permute-start.16 = (bf16[8,192,256]{2,1,0:T(8,128)(2,1)}, bf16[8,192,256]{2,1,0:T(8,128)(2,1)}, u32[]{:S(2)}, u32[]{:S(2)}) collective-permute-start(bf16[8,192,256]{2,1,0:T(8,128)(2,1)} %get-tuple-element.38), channel_id=1, source_target_pairs={{0,8},{8,16},{16,24},{24,0},{32,40},{40,48},{48,56},{56,32},{64,72... | collective-permute-start | bytes 2359304 | tf_op jit(solution)/shard_map/ppermute | solution.py:531
  107.8 34.8 %collective-permute-start.17 = (bf16[8,192,256]{2,1,0:T(8,128)(2,1)}, bf16[8,192,256]{2,1,0:T(8,128)(2,1)}, u32[]{:S(2)}, u32[]{:S(2)}) collective-permute-start(bf16[8,192,256]{2,1,0:T(8,128)(2,1)} %get-tuple-element.39), channel_id=1, source_target_pairs={{0,16},{8,24},{16,0},{24,8},{32,48},{40,56},{48,32},{56,40},{64,80... | collective-permute-start | bytes 2359304 | tf_op jit(solution)/shard_map/ppermute | solution.py:531
  108.8 34.5 %copy-start.8 = (bf16[8,192,256]{2,1,0:T(8,128)(2,1)}, bf16[8,192,256]{2,1,0:T(8,128)(2,1)S(1)}, u32[]{:S(2)}) copy-start(bf16[8,192,256]{2,1,0:T(8,128)(2,1)S(1)} %collective-permute-done.13.refs_4_) | copy-start | bytes 2359300
  108.8 34.5 %collective-permute-start.18 = (bf16[8,192,256]{2,1,0:T(8,128)(2,1)}, bf16[8,192,256]{2,1,0:T(8,128)(2,1)}, u32[]{:S(2)}, u32[]{:S(2)}) collective-permute-start(bf16[8,192,256]{2,1,0:T(8,128)(2,1)} %get-tuple-element.40), channel_id=1, source_target_pairs={{0,24},{8,0},{16,8},{24,16},{32,56},{40,32},{48,40},{56,48},{64,88... | collective-permute-start | bytes 2359304 | tf_op jit(solution)/shard_map/ppermute | solution.py:531
  (9 other events, 177.5 us)
where the time goes:
time: 148 us; the launch traced here: 147 us
  starting transfers between devices  56.4 us (38%)
  waiting for transfers between devices  43.9 us (30%)
  Pallas kernels  41.3 us (28%)
  local copies, waits for them, and re-layouts  2.74 us (2%)
  between operations  1.52 us (1%)
  other arithmetic  1.5 us (1%)
    ppermute x3, waiting for transfers between devices, per_device(): far_z.append(lax.ppermute(onward[n - 1], 'rows', along(n, 0)))  24 us
    all_to_all x1, starting transfers between devices, per_device(): lax.all_to_all(message.reshape(devices, rows, message_width), 'rows', 0,...  19 us
    pallas_call x1, Pallas kernels, per_device(): pl.pallas_call(project_body, grid_spec=pltpu.PrefetchScalarGridSpec(num_s...  9.6 us
    ppermute x3, starting transfers between devices, per_device(): near_z.append(lax.ppermute(buckets[side + n], 'rows', along(n, 0)))  8.52 us
    all_to_all x1, starting transfers between devices, per_device(): lax.all_to_all(packed, 'rows', 0, 0, tiled=True)  7.73 us
    ppermute x7, starting transfers between devices, per_device(): lax.ppermute(parts[o], 'heads', [(c, (c + o) % columns) for c in range(co...  7.6 us
    pallas_call x1, Pallas kernels, per_device(): pl.pallas_call(functools.partial(self_body, rows, scale), out_shape=shape...  6.41 us
    pallas_call x1, Pallas kernels, per_device(): pl.pallas_call(functools.partial(cross_body, rows, scale), out_shape=shap...  6.21 us
  transfers between devices with their start and end apart: 21, of which 14 were waited for; matrix products, arithmetic and copies ran while one was open for 2% of the time, Pallas kernels for 21%

commit v1 on v0

--- a/solution.py
+++ b/solution.py
@@ -559,8 +559,8 @@
             in_specs=[
                 pl.BlockSpec((rows, width), lambda o, me: (0, 0)),
                 pl.BlockSpec((rows, width), lambda o, me: (0, 0)),
-                pl.BlockSpec((width, part), lambda o, me: (0, lax.rem(me[0] + o, columns))),
-                pl.BlockSpec((width, part), lambda o, me: (0, lax.rem(me[0] + o, columns))),
+                pl.BlockSpec((width, part), lambda o, me: (0, o)),
+                pl.BlockSpec((width, part), lambda o, me: (0, o)),
             ],
             out_specs=pl.BlockSpec((1, 2 * rows, part), lambda o, me: (o, 0, 0)),
         ),
@@ -573,11 +573,8 @@
         compiler_params=pltpu.CompilerParams(vmem_limit_bytes=61 << 20),
         name="project",
     )(my_column, slot_attended, slot_cross, self_output, cross_output)
-    summed = parts[0]
-    for o in range(1, columns):
-        summed = summed + lax.ppermute(
-            parts[o], "heads", [(c, (c + o) % columns) for c in range(columns)]
-        )
+    parts = lax.all_to_all(parts, "heads", 0, 0, tiled=True)
+    summed = jnp.sum(parts, axis=0)
     self_update = (slot_stream.astype(f32) + summed[:rows]).astype(bf16)
     cross_update = (jnp.tanh(cross_gate[0]) * summed[rows:]).astype(bf16)
 

time: 148 us -> 134 us (0.905); the launches traced: 147 us -> 132 us
  waiting for transfers between devices: 43.9 us -> 19.8 us
  starting transfers between devices: 56.4 us -> 66.1 us
    ppermute x3, waiting for transfers between devices: 24 us -> 0.72 us  [per_device(): far_z.append(lax.ppermute(onward[n - 1], 'rows', along(n, 0)))]
    all_to_all x1, starting transfers between devices: 7.73 us -> 20.8 us  [per_device(): lax.all_to_all(packed, 'rows', 0, 0, tiled=True)]
    ppermute x7 -> x0, starting transfers between devices: 7.6 us -> none  [per_device(): lax.ppermute(parts[o], 'heads', [(c, (c + o) % columns) for c in range(co...]
    all_to_all x1, starting transfers between devices: 19 us -> 12.6 us  [per_device(): lax.all_to_all(message.reshape(devices, rows, message_width), 'rows', 0,...]
    ppermute x3, waiting for transfers between devices: 3.64 us -> 9.31 us  [per_device(): near_x.append(lax.ppermute(buckets[n], 'rows', along(0, n)))]
    ppermute x7 -> x0, waiting for transfers between devices: 5.65 us -> none  [per_device(): lax.ppermute(parts[o], 'heads', [(c, (c + o) % columns) for c in range(co...]
    ppermute x3, waiting for transfers between devices: 5.93 us -> 1.18 us  [per_device(): far_x.append(lax.ppermute(onward[side - 1 + n - 1], 'rows', along(0, n)))]
    all_to_all x0 -> x1, starting transfers between devices: none -> 4.47 us  [per_device(): parts = lax.all_to_all(parts, 'heads', 0, 0, tiled=True)]
  transfers between devices with their start and end apart: 21 -> 15, of which waited for: 14 -> 6; matrix products, arithmetic and copies ran while one was open for 2% -> 0% of each run, Pallas kernels for 21% -> 27%
where the time goes in v1:
time: 134 us; the launch traced here: 132 us
  starting transfers between devices  66.1 us (49%)
  Pallas kernels  41.4 us (31%)
  waiting for transfers between devices  19.8 us (15%)
  local copies, waits for them, and re-layouts  2.41 us (2%)
  between operations  1.51 us (1%)
    all_to_all x1, starting transfers between devices, per_device(): lax.all_to_all(packed, 'rows', 0, 0, tiled=True)  20.8 us
    all_to_all x1, starting transfers between devices, per_device(): lax.all_to_all(message.reshape(devices, rows, message_width), 'rows', 0,...  12.6 us
    ppermute x3, starting transfers between devices, per_device(): near_z.append(lax.ppermute(buckets[side + n], 'rows', along(n, 0)))  10.3 us
    pallas_call x1, Pallas kernels, per_device(): pl.pallas_call(project_body, grid_spec=pltpu.PrefetchScalarGridSpec(num_s...  9.57 us
    ppermute x3, waiting for transfers between devices, per_device(): near_x.append(lax.ppermute(buckets[n], 'rows', along(0, n)))  9.31 us
    ppermute x3, starting transfers between devices, per_device(): far_z.append(lax.ppermute(onward[n - 1], 'rows', along(n, 0)))  6.59 us
    pallas_call x1, Pallas kernels, per_device(): pl.pallas_call(functools.partial(self_body, rows, scale), out_shape=shape...  6.42 us
    pallas_call x1, Pallas kernels, per_device(): pl.pallas_call(functools.partial(cross_body, rows, scale), out_shape=shap...  6.21 us
  transfers between devices with their start and end apart: 15, of which 6 were waited for; matrix products, arithmetic and copies ran while one was open for 0% of the time, Pallas kernels for 27%

profile of v1, /device:TPU:0, one launch (start us, length us, event | category | flops | bytes accessed | tf_op | source)
XLA Modules:
  0.0 131.9 jit_solution(6413591448431570377)
XLA Ops:
  0.6 5.7 %own.1 = (bf16[8,192,256]{2,1,0:T(8,128)(2,1)}, bf16[8,192,256]{2,1,0:T(8,128)(2,1)}, bf16[8,192,256]{2,1,0:T(8,128)(2,1)}, bf16[8,192,256]{2,1,0:T(8,128)(2,1)}...) custom-call(s32[6,16]{1,0:T(8,128)} %bitcast.24, ...), custom_call_target="tpu_custom_call" | custom-call | bytes 9437184 | tf_op jit(solution)/shard_map/own/pallas_call | solution.py:434
  7.7 2.9 %collective-permute-start.1 = (bf16[8,192,256]{2,1,0:T(8,128)(2,1)}, bf16[8,192,256]{2,1,0:T(8,128)(2,1)S(1)}, u32[]{:S(2)}, u32[]{:S(2)}) collective-permute-start(bf16[8,192,256]{2,1,0:T(8,128)(2,1)} %get-tuple-element.29), channel_id=1, source_target_pairs={{0,16},{8,24},{16,0},{24,8},{32,48},{40,56},{48,32},{56,40},{64,80... | collective-permute-start | bytes 2359304 | tf_op jit(solution)/shard_map/ppermute | solution.py:482
  10.6 1.4 %collective-permute-start.2 = (bf16[8,192,256]{2,1,0:T(8,128)(2,1)}, bf16[8,192,256]{2,1,0:T(8,128)(2,1)}, u32[]{:S(2)}, u32[]{:S(2)}) collective-permute-start(bf16[8,192,256]{2,1,0:T(8,128)(2,1)} %get-tuple-element.30), channel_id=1, source_target_pairs={{0,24},{8,0},{16,8},{24,16},{32,56},{40,32},{48,40},{56,48},{64,88... | collective-permute-start | bytes 2359304 | tf_op jit(solution)/shard_map/ppermute | solution.py:482
  12.0 2.0 %collective-permute-start.3 = (bf16[8,192,256]{2,1,0:T(8,128)(2,1)}, bf16[8,192,256]{2,1,0:T(8,128)(2,1)}, u32[]{:S(2)}, u32[]{:S(2)}) collective-permute-start(bf16[8,192,256]{2,1,0:T(8,128)(2,1)} %get-tuple-element.32), channel_id=1, source_target_pairs={{0,32},{8,40},{16,48},{24,56},{32,64},{40,72},{48,80},{56,88},{64,... | collective-permute-start | bytes 2359304 | tf_op jit(solution)/shard_map/ppermute | solution.py:483
  14.1 3.5 %collective-permute-start.4 = (bf16[8,192,256]{2,1,0:T(8,128)(2,1)}, bf16[8,192,256]{2,1,0:T(8,128)(2,1)}, u32[]{:S(2)}, u32[]{:S(2)}) collective-permute-start(bf16[8,192,256]{2,1,0:T(8,128)(2,1)} %get-tuple-element.33), channel_id=1, source_target_pairs={{0,64},{8,72},{16,80},{24,88},{32,96},{40,104},{48,112},{56,120},{... | collective-permute-start | bytes 2359304 | tf_op jit(solution)/shard_map/ppermute | solution.py:483
  17.6 9.3 %collective-permute-done.refs_1_ = bf16[8,192,256]{2,1,0:T(8,128)(2,1)S(1)} collective-permute-done((bf16[8,192,256]{2,1,0:T(8,128)(2,1)}, bf16[8,192,256]{2,1,0:T(8,128)(2,1)S(1)}, u32[]{:S(2)}, u32[]{:S(2)}) %collective-permute-start) | collective-permute-done | bytes 786464 | tf_op jit(solution)/shard_map/ppermute | solution.py:482
  26.9 4.7 %collective-permute-start.5 = (bf16[8,192,256]{2,1,0:T(8,128)(2,1)}, bf16[8,192,256]{2,1,0:T(8,128)(2,1)}, u32[]{:S(2)}, u32[]{:S(2)}) collective-permute-start(bf16[8,192,256]{2,1,0:T(8,128)(2,1)} %get-tuple-element.34), channel_id=1, source_target_pairs={{0,96},{8,104},{16,112},{24,120},{32,0},{40,8},{48,16},{56,24},{64... | collective-permute-start | bytes 2359304 | tf_op jit(solution)/shard_map/ppermute | solution.py:483
  31.6 1.8 %pack.1 = bf16[16,16,1152]{2,1,0:T(8,128)(2,1)} custom-call(s32[2,16]{1,0:T(2,128)} %bitcast.17, bf16[16,1024]{1,0:T(8,128)(2,1)} %query_ref.2), custom_call_target="tpu_custom_call" | custom-call | tf_op jit(solution)/shard_map/pack/pallas_call | solution.py:421
  33.4 20.8 %all-to-all-start = ((bf16[16,16,1152]{2,1,0:T(8,128)(2,1)}), bf16[16,16,1152]{2,1,0:T(8,128)(2,1)S(1)}, u32[]{:S(2)}, u32[]{:S(2)}) async-start(bf16[16,16,1152]{2,1,0:T(8,128)(2,1)} %pack.1), calls=%async_computation | async-start | bytes 1179648 | tf_op jit(solution)/shard_map/all_to_all | solution.py:428
  55.1 4.8 %mix.1 = (bf16[8,192,256]{2,1,0:T(8,128)(2,1)}, bf16[8,192,256]{2,1,0:T(8,128)(2,1)}, bf16[8,192,256]{2,1,0:T(8,128)(2,1)}, bf16[8,192,256]{2,1,0:T(8,128)(2,1)}...) custom-call(s32[1]{0:T(128)} %bitcast.me_ref, bf16[8,192,256]{2,1,0:T(8,128)(2,1)} %get-tuple-element.27.refs_0_, ...), custom_call_target="tpu_custom_call" | custom-call | bytes 12582912 | tf_op jit(solution)/shard_map/mix/pallas_call | solution.py:513
  60.0 2.0 %collective-permute-start.6 = (bf16[8,192,256]{2,1,0:T(8,128)(2,1)}, bf16[8,192,256]{2,1,0:T(8,128)(2,1)S(1)}, u32[]{:S(2)}, u32[]{:S(2)}) collective-permute-start(bf16[8,192,256]{2,1,0:T(8,128)(2,1)} %get-tuple-element.35), channel_id=1, source_target_pairs={{0,32},{8,40},{16,48},{24,56},{32,64},{40,72},{48,80},{56,88},{64,... | collective-permute-start | bytes 2359304 | tf_op jit(solution)/shard_map/ppermute | solution.py:530
  62.0 6.4 %attend.1.att_ref = bf16[128,128]{1,0:T(8,128)(2,1)} custom-call(s32[16]{0:T(128)} %len_ref.3, bf16[16,1024]{1,0:T(8,128)(2,1)} %query_ref.3, bf16[16,384,256]{2,1,0:T(8,128)(2,1)} %get-tuple-element.22.whole_ref), custom_call_target="tpu_custom_call" | custom-call | flops 25165824 | bytes 3145728 | tf_op jit(solution)/shard_map/attend/pallas_call | solution.py:459
  69.2 6.2 %cross.1 = bf16[256,1408]{1,0:T(8,128)(2,1)} custom-call(s32[2,16]{1,0:T(2,128)S(1)} %bitcast.18, bf16[256,1152]{1,0:T(8,128)(2,1)S(1)} %bitcast.14, s32[1,256]{1,0:T(1,128)S(1)} %bitcast.20, bf16[16,128,256]{2,1,0:T(8,128)(2,1)S(1)} %bitcast.19, bf16[128,128]{1,0:T(8,128)(2,1)S(1)} %copy-done.1, bf16[16,512]{1,0:T(8,128)(2,1)S(1)} %copy-done.4), custom_call_target="tpu_custom_call" | custom-call | flops 671088640 | bytes 2097152 | tf_op jit(solution)/shard_map/cross/pallas_call | solution.py:487
  75.4 12.6 %all-to-all-start.1 = ((bf16[16,16,1408]{2,1,0:T(8,128)(2,1)}), bf16[16,16,1408]{2,1,0:T(8,128)(2,1)S(1)}, u32[]{:S(2)}, u32[]{:S(2)}) async-start(bf16[16,16,1408]{2,1,0:T(8,128)(2,1)} %bitcast.8), calls=%async_computation.1 | async-start | bytes 1441792 | tf_op jit(solution)/shard_map/all_to_all | solution.py:512
  88.0 3.4 %collective-permute-start.7 = (bf16[8,192,256]{2,1,0:T(8,128)(2,1)}, bf16[8,192,256]{2,1,0:T(8,128)(2,1)}, u32[]{:S(2)}, u32[]{:S(2)}) collective-permute-start(bf16[8,192,256]{2,1,0:T(8,128)(2,1)} %get-tuple-element.36), channel_id=1, source_target_pairs={{0,64},{8,72},{16,80},{24,88},{32,96},{40,104},{48,112},{56,120},{... | collective-permute-start | bytes 2359304 | tf_op jit(solution)/shard_map/ppermute | solution.py:530
  92.6 1.5 %collective-permute-start.9 = (bf16[8,192,256]{2,1,0:T(8,128)(2,1)}, bf16[8,192,256]{2,1,0:T(8,128)(2,1)}, u32[]{:S(2)}, u32[]{:S(2)}) collective-permute-start(bf16[8,192,256]{2,1,0:T(8,128)(2,1)} %get-tuple-element.38), channel_id=1, source_target_pairs={{0,8},{8,16},{16,24},{24,0},{32,40},{40,48},{48,56},{56,32},{64,72... | collective-permute-start | bytes 2359304 | tf_op jit(solution)/shard_map/ppermute | solution.py:531
  94.1 2.7 %collective-permute-start.10 = (bf16[8,192,256]{2,1,0:T(8,128)(2,1)}, bf16[8,192,256]{2,1,0:T(8,128)(2,1)}, u32[]{:S(2)}, u32[]{:S(2)}) collective-permute-start(bf16[8,192,256]{2,1,0:T(8,128)(2,1)} %get-tuple-element.39), channel_id=1, source_target_pairs={{0,16},{8,24},{16,0},{24,8},{32,48},{40,56},{48,32},{56,40},{64,80... | collective-permute-start | bytes 2359304 | tf_op jit(solution)/shard_map/ppermute | solution.py:531
  96.8 1.5 %collective-permute-start.11 = (bf16[8,192,256]{2,1,0:T(8,128)(2,1)}, bf16[8,192,256]{2,1,0:T(8,128)(2,1)}, u32[]{:S(2)}, u32[]{:S(2)}) collective-permute-start(bf16[8,192,256]{2,1,0:T(8,128)(2,1)} %get-tuple-element.40), channel_id=1, source_target_pairs={{0,24},{8,0},{16,8},{24,16},{32,56},{40,32},{48,40},{56,48},{64,88... | collective-permute-start | bytes 2359304 | tf_op jit(solution)/shard_map/ppermute | solution.py:531
  98.2 5.0 %all-to-all-done.1.came_ref = bf16[16,16,1408]{2,1,0:T(8,128)(2,1)S(1)} async-done(((bf16[16,16,1408]{2,1,0:T(8,128)(2,1)}), bf16[16,16,1408]{2,1,0:T(8,128)(2,1)S(1)}, u32[]{:S(2)}, u32[]{:S(2)}) %all-to-all-start.1) | async-done | bytes 720928 | tf_op jit(solution)/shard_map/all_to_all | solution.py:512
  104.1 2.8 %combine.1 = (bf16[16,1024]{1,0:T(8,128)(2,1)}, bf16[16,1024]{1,0:T(8,128)(2,1)}, bf16[16,512]{1,0:T(8,128)(2,1)}, s32[8,128]{1,0:T(8,128)}) custom-call(s32[1]{0:T(128)} %bitcast.me_ref, bf16[256,1152]{1,0:T(8,128)(2,1)} %bitcast.15, bf16[16,16,1408]{2,1,0:T(8,128)(2,1)} %copy-done.8), custom_call_target="tpu_custom_call" | custom-call | flops 1048576 | bytes 1048576 | tf_op jit(solution)/shard_map/combine/pallas_call | solution.py:534
  106.9 9.6 %project.1 = f32[8,32,512]{2,1,0:T(8,128)} custom-call(s32[1]{0:T(128)} %bitcast.9.me_ref, bf16[16,1024]{1,0:T(8,128)(2,1)} %get-tuple-element.24.att_ref, bf16[16,1024]{1,0:T(8,128)(2,1)} %get-tuple-element.25.cross_ref, bf16[1024,4096]{1,0:T(8,128)(2,1)} %self_w_ref.1, bf16[1024,4096]{1,0:T(8,128)(2,1)} %cross_w_ref.1), custom_call_target="tpu_custom_call" | custom-call | flops 268435456 | bytes 16777216 | tf_op jit(solution)/shard_map/project/pallas_call | solution.py:554
  116.4 4.5 %all-to-all-start.2 = ((f32[8,32,512]{2,1,0:T(8,128)}), f32[8,32,512]{2,1,0:T(8,128)S(1)}, u32[]{:S(2)}, u32[]{:S(2)}) async-start(f32[8,32,512]{2,1,0:T(8,128)} %project.1), calls=%async_computation.2 | async-start | bytes 1048576 | tf_op jit(solution)/shard_map/all_to_all | solution.py:576
  123.5 4.2 %place.1 = bf16[16,384,256]{2,1,0:T(8,128)(2,1)} custom-call(s32[8,128]{1,0:T(8,128)} %get-tuple-element.26.source_ref, s32[1]{0:T(128)} %bitcast.me_ref, bf16[8,192,256]{2,1,0:T(8,128)(2,1)} %get-tuple-element.27.refs_0_, bf16[8,192,256]{2,1,0:T(8,128)(2,1)} %copy-done.6, bf16[8,192,256]{2,1,0:T(8,128)(2,1)} %copy-done.7, ...), custom_call_target="tpu_custom_call" | custom-call | bytes 6291456 | tf_op jit(solution)/shard_map/place/pallas_call | solution.py:581
  127.8 3.5 %all-to-all-done.2 = f32[8,32,512]{2,1,0:T(8,128)S(1)} async-done(((f32[8,32,512]{2,1,0:T(8,128)}), f32[8,32,512]{2,1,0:T(8,128)S(1)}, u32[]{:S(2)}, u32[]{:S(2)}) %all-to-all-start.2) | async-done | bytes 524320 | tf_op jit(solution)/shard_map/all_to_all | solution.py:576
  (38 shorter events, 7.7 us)
Async XLA Ops:
  6.3 20.6 %collective-permute-start = (bf16[8,192,256]{2,1,0:T(8,128)(2,1)}, bf16[8,192,256]{2,1,0:T(8,128)(2,1)S(1)}, u32[]{:S(2)}, u32[]{:S(2)}) collective-permute-start(bf16[8,192,256]{2,1,0:T(8,128)(2,1)} %get-tuple-element.28), channel_id=1, source_target_pairs={{0,8},{8,16},{16,24},{24,0},{32,40},{40,48},{48,56},{56,32},{64,72... | collective-permute-start | bytes 2359304 | tf_op jit(solution)/shard_map/ppermute | solution.py:482
  7.7 46.5 %collective-permute-start.1 = (bf16[8,192,256]{2,1,0:T(8,128)(2,1)}, bf16[8,192,256]{2,1,0:T(8,128)(2,1)S(1)}, u32[]{:S(2)}, u32[]{:S(2)}) collective-permute-start(bf16[8,192,256]{2,1,0:T(8,128)(2,1)} %get-tuple-element.29), channel_id=1, source_target_pairs={{0,16},{8,24},{16,0},{24,8},{32,48},{40,56},{48,32},{56,40},{64,80... | collective-permute-start | bytes 2359304 | tf_op jit(solution)/shard_map/ppermute | solution.py:482
  10.6 43.7 %collective-permute-start.2 = (bf16[8,192,256]{2,1,0:T(8,128)(2,1)}, bf16[8,192,256]{2,1,0:T(8,128)(2,1)}, u32[]{:S(2)}, u32[]{:S(2)}) collective-permute-start(bf16[8,192,256]{2,1,0:T(8,128)(2,1)} %get-tuple-element.30), channel_id=1, source_target_pairs={{0,24},{8,0},{16,8},{24,16},{32,56},{40,32},{48,40},{56,48},{64,88... | collective-permute-start | bytes 2359304 | tf_op jit(solution)/shard_map/ppermute | solution.py:482
  12.0 42.2 %collective-permute-start.3 = (bf16[8,192,256]{2,1,0:T(8,128)(2,1)}, bf16[8,192,256]{2,1,0:T(8,128)(2,1)}, u32[]{:S(2)}, u32[]{:S(2)}) collective-permute-start(bf16[8,192,256]{2,1,0:T(8,128)(2,1)} %get-tuple-element.32), channel_id=1, source_target_pairs={{0,32},{8,40},{16,48},{24,56},{32,64},{40,72},{48,80},{56,88},{64,... | collective-permute-start | bytes 2359304 | tf_op jit(solution)/shard_map/ppermute | solution.py:483
  14.1 40.3 %collective-permute-start.4 = (bf16[8,192,256]{2,1,0:T(8,128)(2,1)}, bf16[8,192,256]{2,1,0:T(8,128)(2,1)}, u32[]{:S(2)}, u32[]{:S(2)}) collective-permute-start(bf16[8,192,256]{2,1,0:T(8,128)(2,1)} %get-tuple-element.33), channel_id=1, source_target_pairs={{0,64},{8,72},{16,80},{24,88},{32,96},{40,104},{48,112},{56,120},{... | collective-permute-start | bytes 2359304 | tf_op jit(solution)/shard_map/ppermute | solution.py:483
  26.9 27.5 %copy-start.6 = (bf16[8,192,256]{2,1,0:T(8,128)(2,1)}, bf16[8,192,256]{2,1,0:T(8,128)(2,1)S(1)}, u32[]{:S(2)}) copy-start(bf16[8,192,256]{2,1,0:T(8,128)(2,1)S(1)} %collective-permute-done.refs_1_) | copy-start | bytes 2359300
  26.9 27.5 %collective-permute-start.5 = (bf16[8,192,256]{2,1,0:T(8,128)(2,1)}, bf16[8,192,256]{2,1,0:T(8,128)(2,1)}, u32[]{:S(2)}, u32[]{:S(2)}) collective-permute-start(bf16[8,192,256]{2,1,0:T(8,128)(2,1)} %get-tuple-element.34), channel_id=1, source_target_pairs={{0,96},{8,104},{16,112},{24,120},{32,0},{40,8},{48,16},{56,24},{64... | collective-permute-start | bytes 2359304 | tf_op jit(solution)/shard_map/ppermute | solution.py:483
  33.4 35.0 %all-to-all-start = ((bf16[16,16,1152]{2,1,0:T(8,128)(2,1)}), bf16[16,16,1152]{2,1,0:T(8,128)(2,1)S(1)}, u32[]{:S(2)}, u32[]{:S(2)}) async-start(bf16[16,16,1152]{2,1,0:T(8,128)(2,1)} %pack.1), calls=%async_computation | async-start | bytes 1179648 | tf_op jit(solution)/shard_map/all_to_all | solution.py:428
  54.2 0.9 copy-start.7
  60.0 8.5 %copy-start.2 = (s32[16,2]{0,1:T(2,128)S(1)}, s32[16,2]{0,1:T(2,128)}, u32[]{:S(2)}) copy-start(s32[16,2]{0,1:T(2,128)} %param.19) | copy-start | bytes 388
  60.0 8.5 %copy-start.3 = (bf16[16,128,1,256]{3,1,2,0:T(8,128)(2,1)S(1)}, bf16[16,128,1,256]{3,1,2,0:T(8,128)(2,1)}, u32[]{:S(2)}) copy-start(bf16[16,128,1,256]{3,1,2,0:T(8,128)(2,1)} %param.22) | copy-start | bytes 3145732
  60.0 8.5 %copy-start.4 = (bf16[16,512]{1,0:T(8,128)(2,1)S(1)}, bf16[16,512]{1,0:T(8,128)(2,1)}, u32[]{:S(2)}) copy-start(bf16[16,512]{1,0:T(8,128)(2,1)} %stream_ref.1) | copy-start | bytes 49156
  60.0 8.5 %copy-start.5 = (s32[256]{0:T(256)S(1)}, s32[256]{0:T(256)}, u32[]{:S(2)}) copy-start(s32[256]{0:T(256)} %param.20) | copy-start | bytes 3076
  60.0 36.8 %collective-permute-start.6 = (bf16[8,192,256]{2,1,0:T(8,128)(2,1)}, bf16[8,192,256]{2,1,0:T(8,128)(2,1)S(1)}, u32[]{:S(2)}, u32[]{:S(2)}) collective-permute-start(bf16[8,192,256]{2,1,0:T(8,128)(2,1)} %get-tuple-element.35), channel_id=1, source_target_pairs={{0,32},{8,40},{16,48},{24,56},{32,64},{40,72},{48,80},{56,88},{64,... | collective-permute-start | bytes 2359304 | tf_op jit(solution)/shard_map/ppermute | solution.py:530
  68.4 34.8 %copy-start = (bf16[16,16,1152]{2,1,0:T(8,128)(2,1)}, bf16[16,16,1152]{2,1,0:T(8,128)(2,1)S(1)}, u32[]{:S(2)}) copy-start(bf16[16,16,1152]{2,1,0:T(8,128)(2,1)S(1)} %all-to-all-done) | copy-start | bytes 1769476
  75.4 27.8 %all-to-all-start.1 = ((bf16[16,16,1408]{2,1,0:T(8,128)(2,1)}), bf16[16,16,1408]{2,1,0:T(8,128)(2,1)S(1)}, u32[]{:S(2)}, u32[]{:S(2)}) async-start(bf16[16,16,1408]{2,1,0:T(8,128)(2,1)} %bitcast.8), calls=%async_computation.1 | async-start | bytes 1441792 | tf_op jit(solution)/shard_map/all_to_all | solution.py:512
  88.0 33.6 %collective-permute-start.7 = (bf16[8,192,256]{2,1,0:T(8,128)(2,1)}, bf16[8,192,256]{2,1,0:T(8,128)(2,1)}, u32[]{:S(2)}, u32[]{:S(2)}) collective-permute-start(bf16[8,192,256]{2,1,0:T(8,128)(2,1)} %get-tuple-element.36), channel_id=1, source_target_pairs={{0,64},{8,72},{16,80},{24,88},{32,96},{40,104},{48,112},{56,120},{... | collective-permute-start | bytes 2359304 | tf_op jit(solution)/shard_map/ppermute | solution.py:530
  91.5 30.9 %collective-permute-start.8 = (bf16[8,192,256]{2,1,0:T(8,128)(2,1)}, bf16[8,192,256]{2,1,0:T(8,128)(2,1)}, u32[]{:S(2)}, u32[]{:S(2)}) collective-permute-start(bf16[8,192,256]{2,1,0:T(8,128)(2,1)} %get-tuple-element.37), channel_id=1, source_target_pairs={{0,96},{8,104},{16,112},{24,120},{32,0},{40,8},{48,16},{56,24},{64... | collective-permute-start | bytes 2359304 | tf_op jit(solution)/shard_map/ppermute | solution.py:530
  92.6 29.7 %collective-permute-start.9 = (bf16[8,192,256]{2,1,0:T(8,128)(2,1)}, bf16[8,192,256]{2,1,0:T(8,128)(2,1)}, u32[]{:S(2)}, u32[]{:S(2)}) collective-permute-start(bf16[8,192,256]{2,1,0:T(8,128)(2,1)} %get-tuple-element.38), channel_id=1, source_target_pairs={{0,8},{8,16},{16,24},{24,0},{32,40},{40,48},{48,56},{56,32},{64,72... | collective-permute-start | bytes 2359304 | tf_op jit(solution)/shard_map/ppermute | solution.py:531
  94.1 29.4 %collective-permute-start.10 = (bf16[8,192,256]{2,1,0:T(8,128)(2,1)}, bf16[8,192,256]{2,1,0:T(8,128)(2,1)}, u32[]{:S(2)}, u32[]{:S(2)}) collective-permute-start(bf16[8,192,256]{2,1,0:T(8,128)(2,1)} %get-tuple-element.39), channel_id=1, source_target_pairs={{0,16},{8,24},{16,0},{24,8},{32,48},{40,56},{48,32},{56,40},{64,80... | collective-permute-start | bytes 2359304 | tf_op jit(solution)/shard_map/ppermute | solution.py:531
  96.8 19.7 %copy-start.9 = (bf16[8,192,256]{2,1,0:T(8,128)(2,1)}, bf16[8,192,256]{2,1,0:T(8,128)(2,1)S(1)}, u32[]{:S(2)}) copy-start(bf16[8,192,256]{2,1,0:T(8,128)(2,1)S(1)} %collective-permute-done.6.refs_4_) | copy-start | bytes 2359300
  96.8 26.7 %collective-permute-start.11 = (bf16[8,192,256]{2,1,0:T(8,128)(2,1)}, bf16[8,192,256]{2,1,0:T(8,128)(2,1)}, u32[]{:S(2)}, u32[]{:S(2)}) collective-permute-start(bf16[8,192,256]{2,1,0:T(8,128)(2,1)} %get-tuple-element.40), channel_id=1, source_target_pairs={{0,24},{8,0},{16,8},{24,16},{32,56},{40,32},{48,40},{56,48},{64,88... | collective-permute-start | bytes 2359304 | tf_op jit(solution)/shard_map/ppermute | solution.py:531
  116.4 14.8 %all-to-all-start.2 = ((f32[8,32,512]{2,1,0:T(8,128)}), f32[8,32,512]{2,1,0:T(8,128)S(1)}, u32[]{:S(2)}, u32[]{:S(2)}) async-start(f32[8,32,512]{2,1,0:T(8,128)} %project.1), calls=%async_computation.2 | async-start | bytes 1048576 | tf_op jit(solution)/shard_map/all_to_all | solution.py:576
  123.5 7.8 %copy-start.10 = (bf16[16,512]{1,0:T(8,128)(2,1)S(1)}, bf16[16,512]{1,0:T(8,128)(2,1)}, u32[]{:S(2)}) copy-start(bf16[16,512]{1,0:T(8,128)(2,1)} %get-tuple-element.23) | copy-start | bytes 49156
  (2 other events, 1.6 us)

commit v2 on v1

--- a/solution.py
+++ b/solution.py
@@ -67,10 +67,31 @@
         out_ref[d, :, width : width + LANES] = about
 
 
+def page_copies(rows, pages, page_len, pt_ref, pool, held, in_sem):
+    return [
+        [
+            pltpu.make_async_copy(
+                pool.at[pt_ref[p, r]], held.at[r, pl.ds(p * page_len, page_len)], in_sem.at[r, p]
+            )
+            for p in range(pages)
+        ]
+        for r in range(rows)
+    ]
+
+
+def write_token(r, len_ref, kv_ref, held):
+    length = len_ref[r]
+    base = pl.multiple_of((length // 16) * 16, 16)
+    block = held[r, pl.ds(base, 16), :].astype(f32)
+    token = kv_ref[r : r + 1, :].astype(f32)
+    here = iota(block.shape, 0) == length - base
+    held[r, pl.ds(base, 16), :] = jnp.where(here, token, block).astype(bf16)
+
+
 def own_body(
     rows, pages, page_len, side, pt_ref, len_ref, mig_ref, me_ref, pool, kv_ref, *refs,
 ):
-    across, down, (whole, held, in_sem, across_sem, down_sem, whole_sem) = (
+    across, down, (held, in_sem, across_sem, down_sem) = (
         refs[:side],
         refs[side : 2 * side],
         refs[2 * side :],
@@ -80,10 +101,7 @@
     half = history // 2
     my_z, my_x = me_ref[0] // side, me_ref[0] % side
 
-    def fetching(r, p):
-        return pltpu.make_async_copy(
-            pool.at[pt_ref[p, r]], held.at[r, pl.ds(p * page_len, page_len)], in_sem.at[r, p]
-        )
+    copies = page_copies(rows, pages, page_len, pt_ref, pool, held, in_sem)
 
     def send(r):
         to_z, to_x = targets[r] // side, targets[r] % side
@@ -104,23 +122,14 @@
                 ).start()
 
     for r in range(rows):
-        for p in range(pages):
-            fetching(r, p).start()
-    for r in range(rows):
-        for p in range(pages):
-            fetching(r, p).wait()
-        length = len_ref[r]
-        base = pl.multiple_of((length // 16) * 16, 16)
-        block = held[r, pl.ds(base, 16), :].astype(f32)
-        token = kv_ref[r : r + 1, :].astype(f32)
-        here = iota(block.shape, 0) == length - base
-        held[r, pl.ds(base, 16), :] = jnp.where(here, token, block).astype(bf16)
-
+        for copy in copies[r]:
+            copy.start()
+    for r in range(rows):
+        for copy in copies[r]:
+            copy.wait()
+        write_token(r, len_ref, kv_ref, held)
         send(r)
-        pltpu.make_async_copy(held.at[r], whole.at[r], whole_sem.at[r]).start()
-
-    for r in range(rows):
-        pltpu.make_async_copy(held.at[r], whole.at[r], whole_sem.at[r]).wait()
+
     for r in range(rows):
 
         @pl.when(targets[r] >= 0)
@@ -133,21 +142,32 @@
             ).wait()
 
 
-def self_body(rows, scale, len_ref, query_ref, whole_ref, att_ref, split_ref):
-    _, history, both = whole_ref.shape
+def self_body(
+    rows, pages, page_len, scale, pt_ref, len_ref, pool, kv_ref, query_ref, att_ref, held,
+    split_ref, in_sem,
+):
+    _, history, both = held.shape
     head = both // 2
     heads = query_ref.shape[1] // head
+    copies = page_copies(rows, pages, page_len, pt_ref, pool, held, in_sem)
+    for r in range(rows):
+        for copy in copies[r]:
+            copy.start()
     for h in range(heads):
         split_ref[pl.ds(h, rows, stride=heads), :] = query_ref[:, h * head : (h + 1) * head].astype(
             f32
         )
     for r in range(rows):
+        for copy in copies[r]:
+            copy.wait()
+        write_token(r, len_ref, kv_ref, held)
+    for r in range(rows):
         queries = split_ref[r * heads : (r + 1) * heads, :].astype(bf16)
-        scores = against(queries, whole_ref[r, :, 0:head]) * scale
+        scores = against(queries, held[r, :, 0:head]) * scale
         scores = jnp.where(iota((heads, history), 1) <= len_ref[r], scores, very_low)
         weights = jnp.exp(scores - jnp.max(scores, axis=1, keepdims=True))
         total = jnp.sum(weights, axis=1, keepdims=True)
-        blended = jnp.dot(weights.astype(bf16), whole_ref[r, :, head:], preferred_element_type=f32)
+        blended = jnp.dot(weights.astype(bf16), held[r, :, head:], preferred_element_type=f32)
         att_ref[r * heads : (r + 1) * heads, :] = (blended / total).astype(bf16)
 
 
@@ -431,21 +451,20 @@
     shifts = (1, *range(side - 1, 1, -1))
     half = history // 2
     bucket = shape((2 * side, half, both), bf16)
-    *buckets, whole = pl.pallas_call(
+    buckets = pl.pallas_call(
         functools.partial(own_body, rows, pages, page_len, side),
-        out_shape=(*([bucket] * (2 * side)), shape((rows, history, both), bf16)),
+        out_shape=[bucket] * (2 * side),
         in_specs=[smem(), smem(), smem(), smem(), anywhere(), vmem()],
-        out_specs=(*([anywhere()] * (2 * side)), anywhere()),
+        out_specs=[anywhere()] * (2 * side),
         scratch_shapes=[
             VMEM((rows, history, both), bf16),
             pltpu.SemaphoreType.DMA((rows, pages)),
             pltpu.SemaphoreType.DMA((rows,)),
             pltpu.SemaphoreType.DMA((rows,)),
-            pltpu.SemaphoreType.DMA((rows,)),
         ],
         compiler_params=pltpu.CompilerParams(vmem_limit_bytes=61 << 20),
         cost_estimate=pl.CostEstimate(
-            flops=0, bytes_accessed=6 * rows * history * both, transcendentals=0
+            flops=0, bytes_accessed=4 * rows * history * both, transcendentals=0
         ),
         name="own",
     )(
@@ -457,18 +476,29 @@
         new_kv.reshape(rows, both),
     )
     attended = pl.pallas_call(
-        functools.partial(self_body, rows, scale),
+        functools.partial(self_body, rows, pages, page_len, scale),
         out_shape=shape((rows * heads, head), bf16),
-        in_specs=[smem(), vmem(), vmem()],
+        in_specs=[smem(), smem(), anywhere(), vmem(), vmem()],
         out_specs=vmem(),
-        scratch_shapes=[VMEM((rows * heads, head), f32)],
+        scratch_shapes=[
+            VMEM((rows, history, both), bf16),
+            VMEM((rows * heads, head), f32),
+            pltpu.SemaphoreType.DMA((rows, pages)),
+        ],
+        compiler_params=pltpu.CompilerParams(vmem_limit_bytes=61 << 20),
         cost_estimate=pl.CostEstimate(
             flops=4 * rows * heads * history * head,
             bytes_accessed=2 * rows * history * both,
             transcendentals=rows * heads * history,
         ),
         name="attend",
-    )(lengths, self_query, whole)
+    )(
+        page_table.T,
+        lengths,
+        cache_pool.reshape(pool_pages, page_len, both),
+        new_kv.reshape(rows, both),
+        self_query,
+    )
 
     def along(dz, dx):
         return [
@@ -499,7 +529,7 @@
             bytes_accessed=2 * images * tokens * both + 4 * everyone * width,
             transcendentals=everyone * heads * tokens,
         ),
-        compiler_params=pltpu.CompilerParams(vmem_limit_bytes=40 << 20),
+        compiler_params=pltpu.CompilerParams(vmem_limit_bytes=67_000_000),
         name="cross",
     )(
         mig,
@@ -547,7 +577,7 @@
             bytes_accessed=4 * everyone * width,
             transcendentals=everyone * LANES,
         ),
-        compiler_params=pltpu.CompilerParams(vmem_limit_bytes=61 << 20),
+        compiler_params=pltpu.CompilerParams(vmem_limit_bytes=67_000_000),
         name="combine",
     )(my_row, asked, came)
 
@@ -570,7 +600,7 @@
             bytes_accessed=4 * width * out_width,
             transcendentals=0,
         ),
-        compiler_params=pltpu.CompilerParams(vmem_limit_bytes=61 << 20),
+        compiler_params=pltpu.CompilerParams(vmem_limit_bytes=67_000_000),
         name="project",
     )(my_column, slot_attended, slot_cross, self_output, cross_output)
     parts = lax.all_to_all(parts, "heads", 0, 0, tiled=True)

time: 134 us -> 134 us (level)
  Pallas kernels: 41.4 us -> 43 us
    pallas_call x1, Pallas kernels: 6.42 us -> 7.95 us  [per_device(): pl.pallas_call(functools.partial(self_body, rows, pages, page_len, scale)...]
  transfers between devices with their start and end apart: 15 -> 15, of which waited for: 6 -> 5; matrix products, arithmetic and copies ran while one was open for 0% -> 0% of each run, Pallas kernels for 27% -> 29%
where the time goes in v2:
time: 134 us; the launch traced here: 132 us
  starting transfers between devices  66.2 us (49%)
  Pallas kernels  43 us (32%)
  waiting for transfers between devices  19.8 us (15%)
  between operations  1.49 us (1%)
  local copies, waits for them, and re-layouts  1.34 us (1%)
    all_to_all x1, starting transfers between devices, per_device(): lax.all_to_all(packed, 'rows', 0, 0, tiled=True)  21.3 us
    all_to_all x1, starting transfers between devices, per_device(): lax.all_to_all(message.reshape(devices, rows, message_width), 'rows', 0,...  12.1 us
    ppermute x3, starting transfers between devices, per_device(): near_z.append(lax.ppermute(buckets[side + n], 'rows', along(n, 0)))  10.2 us
    pallas_call x1, Pallas kernels, per_device(): pl.pallas_call(project_body, grid_spec=pltpu.PrefetchScalarGridSpec(num_s...  9.57 us
    ppermute x3, waiting for transfers between devices, per_device(): near_x.append(lax.ppermute(buckets[n], 'rows', along(0, n)))  9.17 us
    pallas_call x1, Pallas kernels, per_device(): pl.pallas_call(functools.partial(self_body, rows, pages, page_len, scale)...  7.95 us
    pallas_call x1, Pallas kernels, per_device(): pl.pallas_call(functools.partial(cross_body, rows, scale), out_shape=shap...  7.12 us
    ppermute x3, starting transfers between devices, per_device(): far_z.append(lax.ppermute(onward[n - 1], 'rows', along(n, 0)))  6.5 us
  transfers between devices with their start and end apart: 15, of which 5 were waited for; matrix products, arithmetic and copies ran while one was open for 0% of the time, Pallas kernels for 29%

profile of v2, /device:TPU:0, one launch (start us, length us, event | category | flops | bytes accessed | tf_op | source)
XLA Modules:
  0.0 132.4 jit_solution(975190954033344665)
XLA Ops:
  0.6 4.9 %own.1 = (bf16[8,192,256]{2,1,0:T(8,128)(2,1)}, bf16[8,192,256]{2,1,0:T(8,128)(2,1)}, bf16[8,192,256]{2,1,0:T(8,128)(2,1)}, bf16[8,192,256]{2,1,0:T(8,128)(2,1)}...) custom-call(s32[6,16]{1,0:T(8,128)} %bitcast.20, ...), custom_call_target="tpu_custom_call" | custom-call | bytes 6291456 | tf_op jit(solution)/shard_map/own/pallas_call | solution.py:454
  5.6 1.5 %collective-permute-start = (bf16[8,192,256]{2,1,0:T(8,128)(2,1)}, bf16[8,192,256]{2,1,0:T(8,128)(2,1)S(1)}, u32[]{:S(2)}, u32[]{:S(2)}) collective-permute-start(bf16[8,192,256]{2,1,0:T(8,128)(2,1)} %get-tuple-element.26), channel_id=1, source_target_pairs={{0,8},{8,16},{16,24},{24,0},{32,40},{40,48},{48,56},{56,32},{64,72... | collective-permute-start | bytes 2359304 | tf_op jit(solution)/shard_map/ppermute | solution.py:512
  7.1 2.7 %collective-permute-start.1 = (bf16[8,192,256]{2,1,0:T(8,128)(2,1)}, bf16[8,192,256]{2,1,0:T(8,128)(2,1)S(1)}, u32[]{:S(2)}, u32[]{:S(2)}) collective-permute-start(bf16[8,192,256]{2,1,0:T(8,128)(2,1)} %get-tuple-element.27), channel_id=1, source_target_pairs={{0,16},{8,24},{16,0},{24,8},{32,48},{40,56},{48,32},{56,40},{64,80... | collective-permute-start | bytes 2359304 | tf_op jit(solution)/shard_map/ppermute | solution.py:512
  9.8 1.6 %collective-permute-start.2 = (bf16[8,192,256]{2,1,0:T(8,128)(2,1)}, bf16[8,192,256]{2,1,0:T(8,128)(2,1)S(1)}, u32[]{:S(2)}, u32[]{:S(2)}) collective-permute-start(bf16[8,192,256]{2,1,0:T(8,128)(2,1)} %get-tuple-element.28), channel_id=1, source_target_pairs={{0,24},{8,0},{16,8},{24,16},{32,56},{40,32},{48,40},{56,48},{64,88... | collective-permute-start | bytes 2359304 | tf_op jit(solution)/shard_map/ppermute | solution.py:512
  11.4 1.9 %collective-permute-start.3 = (bf16[8,192,256]{2,1,0:T(8,128)(2,1)}, bf16[8,192,256]{2,1,0:T(8,128)(2,1)S(1)}, u32[]{:S(2)}, u32[]{:S(2)}) collective-permute-start(bf16[8,192,256]{2,1,0:T(8,128)(2,1)} %get-tuple-element.30), channel_id=1, source_target_pairs={{0,32},{8,40},{16,48},{24,56},{32,64},{40,72},{48,80},{56,88},{64,... | collective-permute-start | bytes 2359304 | tf_op jit(solution)/shard_map/ppermute | solution.py:513
  13.3 3.6 %collective-permute-start.4 = (bf16[8,192,256]{2,1,0:T(8,128)(2,1)}, bf16[8,192,256]{2,1,0:T(8,128)(2,1)}, u32[]{:S(2)}, u32[]{:S(2)}) collective-permute-start(bf16[8,192,256]{2,1,0:T(8,128)(2,1)} %get-tuple-element.31), channel_id=1, source_target_pairs={{0,64},{8,72},{16,80},{24,88},{32,96},{40,104},{48,112},{56,120},{... | collective-permute-start | bytes 2359304 | tf_op jit(solution)/shard_map/ppermute | solution.py:513
  16.9 9.2 %collective-permute-done.refs_1_ = bf16[8,192,256]{2,1,0:T(8,128)(2,1)S(1)} collective-permute-done((bf16[8,192,256]{2,1,0:T(8,128)(2,1)}, bf16[8,192,256]{2,1,0:T(8,128)(2,1)S(1)}, u32[]{:S(2)}, u32[]{:S(2)}) %collective-permute-start) | collective-permute-done | bytes 786464 | tf_op jit(solution)/shard_map/ppermute | solution.py:512
  26.1 4.7 %collective-permute-start.5 = (bf16[8,192,256]{2,1,0:T(8,128)(2,1)}, bf16[8,192,256]{2,1,0:T(8,128)(2,1)}, u32[]{:S(2)}, u32[]{:S(2)}) collective-permute-start(bf16[8,192,256]{2,1,0:T(8,128)(2,1)} %get-tuple-element.32), channel_id=1, source_target_pairs={{0,96},{8,104},{16,112},{24,120},{32,0},{40,8},{48,16},{56,24},{64... | collective-permute-start | bytes 2359304 | tf_op jit(solution)/shard_map/ppermute | solution.py:513
  30.8 1.8 %pack.1 = bf16[16,16,1152]{2,1,0:T(8,128)(2,1)} custom-call(s32[2,16]{1,0:T(2,128)} %bitcast.23, bf16[16,1024]{1,0:T(8,128)(2,1)} %query_ref.2), custom_call_target="tpu_custom_call" | custom-call | tf_op jit(solution)/shard_map/pack/pallas_call | solution.py:441
  32.6 21.3 %all-to-all-start = ((bf16[16,16,1152]{2,1,0:T(8,128)(2,1)}), bf16[16,16,1152]{2,1,0:T(8,128)(2,1)}, u32[]{:S(2)}, u32[]{:S(2)}) async-start(bf16[16,16,1152]{2,1,0:T(8,128)(2,1)} %pack.1), calls=%async_computation | async-start | bytes 1179648 | tf_op jit(solution)/shard_map/all_to_all | solution.py:448
  55.3 4.8 %mix.1 = (bf16[8,192,256]{2,1,0:T(8,128)(2,1)}, bf16[8,192,256]{2,1,0:T(8,128)(2,1)}, bf16[8,192,256]{2,1,0:T(8,128)(2,1)}, bf16[8,192,256]{2,1,0:T(8,128)(2,1)}...) custom-call(s32[1]{0:T(128)} %bitcast.me_ref, bf16[8,192,256]{2,1,0:T(8,128)(2,1)} %get-tuple-element.25.refs_0_, ...), custom_call_target="tpu_custom_call" | custom-call | bytes 12582912 | tf_op jit(solution)/shard_map/mix/pallas_call | solution.py:543
  60.1 1.9 %collective-permute-start.6 = (bf16[8,192,256]{2,1,0:T(8,128)(2,1)}, bf16[8,192,256]{2,1,0:T(8,128)(2,1)}, u32[]{:S(2)}, u32[]{:S(2)}) collective-permute-start(bf16[8,192,256]{2,1,0:T(8,128)(2,1)} %get-tuple-element.33), channel_id=1, source_target_pairs={{0,32},{8,40},{16,48},{24,56},{32,64},{40,72},{48,80},{56,88},{64,... | collective-permute-start | bytes 2359304 | tf_op jit(solution)/shard_map/ppermute | solution.py:560
  62.0 8.0 %attend.1.att_ref = bf16[128,128]{1,0:T(8,128)(2,1)} custom-call(s32[6,16]{1,0:T(8,128)} %bitcast.21, s32[16]{0:T(128)} %len_ref.3, bf16[96,64,256]{2,1,0:T(8,128)(2,1)} %bitcast.15, bf16[16,256]{1,0:T(8,128)(2,1)} %bitcast.19, bf16[16,1024]{1,0:T(8,128)(2,1)} %query_ref.3), custom_call_target="tpu_custom_call" | custom-call | flops 25165824 | bytes 3145728 | tf_op jit(solution)/shard_map/attend/pallas_call | solution.py:478
  70.0 7.1 %cross.1 = bf16[256,1408]{1,0:T(8,128)(2,1)} custom-call(s32[2,16]{1,0:T(2,128)} %bitcast.24, bf16[256,1152]{1,0:T(8,128)(2,1)} %bitcast.2.asked_ref, s32[1,256]{1,0:T(1,128)} %bitcast.26, bf16[16,128,256]{2,1,0:T(8,128)(2,1)} %bitcast.25, bf16[128,128]{1,0:T(8,128)(2,1)} %attend.1.att_ref, bf16[16,512]{1,0:T(8,128)(2,1)} %stream_ref.1), custom_call_target="tpu_custom_call" | custom-call | flops 671088640 | bytes 2097152 | tf_op jit(solution)/shard_map/cross/pallas_call | solution.py:517
  77.1 12.1 %all-to-all-start.1 = ((bf16[16,16,1408]{2,1,0:T(8,128)(2,1)}), bf16[16,16,1408]{2,1,0:T(8,128)(2,1)}, u32[]{:S(2)}, u32[]{:S(2)}) async-start(bf16[16,16,1408]{2,1,0:T(8,128)(2,1)} %bitcast.17), calls=%async_computation.1 | async-start | bytes 1441792 | tf_op jit(solution)/shard_map/all_to_all | solution.py:542
  89.3 3.4 %collective-permute-start.7 = (bf16[8,192,256]{2,1,0:T(8,128)(2,1)}, bf16[8,192,256]{2,1,0:T(8,128)(2,1)}, u32[]{:S(2)}, u32[]{:S(2)}) collective-permute-start(bf16[8,192,256]{2,1,0:T(8,128)(2,1)} %get-tuple-element.34), channel_id=1, source_target_pairs={{0,64},{8,72},{16,80},{24,88},{32,96},{40,104},{48,112},{56,120},{... | collective-permute-start | bytes 2359304 | tf_op jit(solution)/shard_map/ppermute | solution.py:560
  95.3 2.7 %collective-permute-start.10 = (bf16[8,192,256]{2,1,0:T(8,128)(2,1)}, bf16[8,192,256]{2,1,0:T(8,128)(2,1)}, u32[]{:S(2)}, u32[]{:S(2)}) collective-permute-start(bf16[8,192,256]{2,1,0:T(8,128)(2,1)} %get-tuple-element.37), channel_id=1, source_target_pairs={{0,16},{8,24},{16,0},{24,8},{32,48},{40,56},{48,32},{56,40},{64,80... | collective-permute-start | bytes 2359304 | tf_op jit(solution)/shard_map/ppermute | solution.py:561
  99.4 5.1 %all-to-all-done.1.came_ref = bf16[16,16,1408]{2,1,0:T(8,128)(2,1)} async-done(((bf16[16,16,1408]{2,1,0:T(8,128)(2,1)}), bf16[16,16,1408]{2,1,0:T(8,128)(2,1)}, u32[]{:S(2)}, u32[]{:S(2)}) %all-to-all-start.1) | async-done | bytes 720928 | tf_op jit(solution)/shard_map/all_to_all | solution.py:542
  104.5 2.8 %combine.1 = (bf16[16,1024]{1,0:T(8,128)(2,1)}, bf16[16,1024]{1,0:T(8,128)(2,1)}, bf16[16,512]{1,0:T(8,128)(2,1)}, s32[8,128]{1,0:T(8,128)}) custom-call(s32[1]{0:T(128)} %bitcast.me_ref, bf16[256,1152]{1,0:T(8,128)(2,1)} %bitcast.2.asked_ref, bf16[16,16,1408]{2,1,0:T(8,128)(2,1)} %all-to-all-done.1.came_ref), custom_call_target="tpu_custom_call" | custom-call | flops 1048576 | bytes 1048576 | tf_op jit(solution)/shard_map/combine/pallas_call | solution.py:564
  107.3 9.6 %project.1 = f32[8,32,512]{2,1,0:T(8,128)} custom-call(s32[1]{0:T(128)} %bitcast.9.me_ref, bf16[16,1024]{1,0:T(8,128)(2,1)} %get-tuple-element.22.att_ref, bf16[16,1024]{1,0:T(8,128)(2,1)} %get-tuple-element.23.cross_ref, bf16[1024,4096]{1,0:T(8,128)(2,1)} %self_w_ref.1, bf16[1024,4096]{1,0:T(8,128)(2,1)} %cross_w_ref.1), custom_call_target="tpu_custom_call" | custom-call | flops 268435456 | bytes 16777216 | tf_op jit(solution)/shard_map/project/pallas_call | solution.py:584
  116.9 4.6 %all-to-all-start.2 = ((f32[8,32,512]{2,1,0:T(8,128)}), f32[8,32,512]{2,1,0:T(8,128)S(1)}, u32[]{:S(2)}, u32[]{:S(2)}) async-start(f32[8,32,512]{2,1,0:T(8,128)} %project.1), calls=%async_computation.2 | async-start | bytes 1048576 | tf_op jit(solution)/shard_map/all_to_all | solution.py:606
  122.2 1.5 %collective-permute-done.8.refs_6_ = bf16[8,192,256]{2,1,0:T(8,128)(2,1)} collective-permute-done((bf16[8,192,256]{2,1,0:T(8,128)(2,1)}, bf16[8,192,256]{2,1,0:T(8,128)(2,1)}, u32[]{:S(2)}, u32[]{:S(2)}) %collective-permute-start.8) | collective-permute-done | bytes 786464 | tf_op jit(solution)/shard_map/ppermute | solution.py:560
  124.8 4.1 %place.1 = bf16[16,384,256]{2,1,0:T(8,128)(2,1)} custom-call(s32[8,128]{1,0:T(8,128)} %get-tuple-element.24.source_ref, s32[1]{0:T(128)} %bitcast.me_ref, bf16[8,192,256]{2,1,0:T(8,128)(2,1)} %get-tuple-element.25.refs_0_, bf16[8,192,256]{2,1,0:T(8,128)(2,1)} %copy-done, bf16[8,192,256]{2,1,0:T(8,128)(2,1)} %copy-done.1, bf16[8,192,256]{2,1,0:T(8,128)(2,1)} %copy-done.2, ...), custom_call_target="tpu_custom_call" | custom-call | bytes 6291456 | tf_op jit(solution)/shard_map/place/pallas_call | solution.py:611
  129.0 2.8 %all-to-all-done.2 = f32[8,32,512]{2,1,0:T(8,128)S(1)} async-done(((f32[8,32,512]{2,1,0:T(8,128)}), f32[8,32,512]{2,1,0:T(8,128)S(1)}, u32[]{:S(2)}, u32[]{:S(2)}) %all-to-all-start.2) | async-done | bytes 524320 | tf_op jit(solution)/shard_map/all_to_all | solution.py:606
  (26 shorter events, 7.3 us)
Async XLA Ops:
  5.6 20.5 %collective-permute-start = (bf16[8,192,256]{2,1,0:T(8,128)(2,1)}, bf16[8,192,256]{2,1,0:T(8,128)(2,1)S(1)}, u32[]{:S(2)}, u32[]{:S(2)}) collective-permute-start(bf16[8,192,256]{2,1,0:T(8,128)(2,1)} %get-tuple-element.26), channel_id=1, source_target_pairs={{0,8},{8,16},{16,24},{24,0},{32,40},{40,48},{48,56},{56,32},{64,72... | collective-permute-start | bytes 2359304 | tf_op jit(solution)/shard_map/ppermute | solution.py:512
  7.1 46.8 %collective-permute-start.1 = (bf16[8,192,256]{2,1,0:T(8,128)(2,1)}, bf16[8,192,256]{2,1,0:T(8,128)(2,1)S(1)}, u32[]{:S(2)}, u32[]{:S(2)}) collective-permute-start(bf16[8,192,256]{2,1,0:T(8,128)(2,1)} %get-tuple-element.27), channel_id=1, source_target_pairs={{0,16},{8,24},{16,0},{24,8},{32,48},{40,56},{48,32},{56,40},{64,80... | collective-permute-start | bytes 2359304 | tf_op jit(solution)/shard_map/ppermute | solution.py:512
  9.8 44.1 %collective-permute-start.2 = (bf16[8,192,256]{2,1,0:T(8,128)(2,1)}, bf16[8,192,256]{2,1,0:T(8,128)(2,1)S(1)}, u32[]{:S(2)}, u32[]{:S(2)}) collective-permute-start(bf16[8,192,256]{2,1,0:T(8,128)(2,1)} %get-tuple-element.28), channel_id=1, source_target_pairs={{0,24},{8,0},{16,8},{24,16},{32,56},{40,32},{48,40},{56,48},{64,88... | collective-permute-start | bytes 2359304 | tf_op jit(solution)/shard_map/ppermute | solution.py:512
  11.4 42.5 %collective-permute-start.3 = (bf16[8,192,256]{2,1,0:T(8,128)(2,1)}, bf16[8,192,256]{2,1,0:T(8,128)(2,1)S(1)}, u32[]{:S(2)}, u32[]{:S(2)}) collective-permute-start(bf16[8,192,256]{2,1,0:T(8,128)(2,1)} %get-tuple-element.30), channel_id=1, source_target_pairs={{0,32},{8,40},{16,48},{24,56},{32,64},{40,72},{48,80},{56,88},{64,... | collective-permute-start | bytes 2359304 | tf_op jit(solution)/shard_map/ppermute | solution.py:513
  13.3 40.6 %collective-permute-start.4 = (bf16[8,192,256]{2,1,0:T(8,128)(2,1)}, bf16[8,192,256]{2,1,0:T(8,128)(2,1)}, u32[]{:S(2)}, u32[]{:S(2)}) collective-permute-start(bf16[8,192,256]{2,1,0:T(8,128)(2,1)} %get-tuple-element.31), channel_id=1, source_target_pairs={{0,64},{8,72},{16,80},{24,88},{32,96},{40,104},{48,112},{56,120},{... | collective-permute-start | bytes 2359304 | tf_op jit(solution)/shard_map/ppermute | solution.py:513
  26.1 27.9 %copy-start = (bf16[8,192,256]{2,1,0:T(8,128)(2,1)}, bf16[8,192,256]{2,1,0:T(8,128)(2,1)S(1)}, u32[]{:S(2)}) copy-start(bf16[8,192,256]{2,1,0:T(8,128)(2,1)S(1)} %collective-permute-done.refs_1_) | copy-start | bytes 2359300
  26.1 27.9 %collective-permute-start.5 = (bf16[8,192,256]{2,1,0:T(8,128)(2,1)}, bf16[8,192,256]{2,1,0:T(8,128)(2,1)}, u32[]{:S(2)}, u32[]{:S(2)}) collective-permute-start(bf16[8,192,256]{2,1,0:T(8,128)(2,1)} %get-tuple-element.32), channel_id=1, source_target_pairs={{0,96},{8,104},{16,112},{24,120},{32,0},{40,8},{48,16},{56,24},{64... | collective-permute-start | bytes 2359304 | tf_op jit(solution)/shard_map/ppermute | solution.py:513
  32.6 37.4 %all-to-all-start = ((bf16[16,16,1152]{2,1,0:T(8,128)(2,1)}), bf16[16,16,1152]{2,1,0:T(8,128)(2,1)}, u32[]{:S(2)}, u32[]{:S(2)}) async-start(bf16[16,16,1152]{2,1,0:T(8,128)(2,1)} %pack.1), calls=%async_computation | async-start | bytes 1179648 | tf_op jit(solution)/shard_map/all_to_all | solution.py:448
  53.9 0.9 copy-start.1
  53.9 1.1 copy-start.2
  53.9 1.4 %copy-start.3 = (bf16[8,192,256]{2,1,0:T(8,128)(2,1)}, bf16[8,192,256]{2,1,0:T(8,128)(2,1)S(1)}, u32[]{:S(2)}) copy-start(bf16[8,192,256]{2,1,0:T(8,128)(2,1)S(1)} %collective-permute-done.3.refs_5_.refs_8_) | copy-start | bytes 2359300
  60.1 37.9 %collective-permute-start.6 = (bf16[8,192,256]{2,1,0:T(8,128)(2,1)}, bf16[8,192,256]{2,1,0:T(8,128)(2,1)}, u32[]{:S(2)}, u32[]{:S(2)}) collective-permute-start(bf16[8,192,256]{2,1,0:T(8,128)(2,1)} %get-tuple-element.33), channel_id=1, source_target_pairs={{0,32},{8,40},{16,48},{24,56},{32,64},{40,72},{48,80},{56,88},{64,... | collective-permute-start | bytes 2359304 | tf_op jit(solution)/shard_map/ppermute | solution.py:560
  77.1 27.4 %all-to-all-start.1 = ((bf16[16,16,1408]{2,1,0:T(8,128)(2,1)}), bf16[16,16,1408]{2,1,0:T(8,128)(2,1)}, u32[]{:S(2)}, u32[]{:S(2)}) async-start(bf16[16,16,1408]{2,1,0:T(8,128)(2,1)} %bitcast.17), calls=%async_computation.1 | async-start | bytes 1441792 | tf_op jit(solution)/shard_map/all_to_all | solution.py:542
  89.3 32.9 %collective-permute-start.7 = (bf16[8,192,256]{2,1,0:T(8,128)(2,1)}, bf16[8,192,256]{2,1,0:T(8,128)(2,1)}, u32[]{:S(2)}, u32[]{:S(2)}) collective-permute-start(bf16[8,192,256]{2,1,0:T(8,128)(2,1)} %get-tuple-element.34), channel_id=1, source_target_pairs={{0,64},{8,72},{16,80},{24,88},{32,96},{40,104},{48,112},{56,120},{... | collective-permute-start | bytes 2359304 | tf_op jit(solution)/shard_map/ppermute | solution.py:560
  92.6 31.0 %collective-permute-start.8 = (bf16[8,192,256]{2,1,0:T(8,128)(2,1)}, bf16[8,192,256]{2,1,0:T(8,128)(2,1)}, u32[]{:S(2)}, u32[]{:S(2)}) collective-permute-start(bf16[8,192,256]{2,1,0:T(8,128)(2,1)} %get-tuple-element.35), channel_id=1, source_target_pairs={{0,96},{8,104},{16,112},{24,120},{32,0},{40,8},{48,16},{56,24},{64... | collective-permute-start | bytes 2359304 | tf_op jit(solution)/shard_map/ppermute | solution.py:560
  93.8 29.9 %collective-permute-start.9 = (bf16[8,192,256]{2,1,0:T(8,128)(2,1)}, bf16[8,192,256]{2,1,0:T(8,128)(2,1)}, u32[]{:S(2)}, u32[]{:S(2)}) collective-permute-start(bf16[8,192,256]{2,1,0:T(8,128)(2,1)} %get-tuple-element.36), channel_id=1, source_target_pairs={{0,8},{8,16},{16,24},{24,0},{32,40},{40,48},{48,56},{56,32},{64,72... | collective-permute-start | bytes 2359304 | tf_op jit(solution)/shard_map/ppermute | solution.py:561
  95.3 29.6 %collective-permute-start.10 = (bf16[8,192,256]{2,1,0:T(8,128)(2,1)}, bf16[8,192,256]{2,1,0:T(8,128)(2,1)}, u32[]{:S(2)}, u32[]{:S(2)}) collective-permute-start(bf16[8,192,256]{2,1,0:T(8,128)(2,1)} %get-tuple-element.37), channel_id=1, source_target_pairs={{0,16},{8,24},{16,0},{24,8},{32,48},{40,56},{48,32},{56,40},{64,80... | collective-permute-start | bytes 2359304 | tf_op jit(solution)/shard_map/ppermute | solution.py:561
  98.0 26.9 %collective-permute-start.11 = (bf16[8,192,256]{2,1,0:T(8,128)(2,1)}, bf16[8,192,256]{2,1,0:T(8,128)(2,1)}, u32[]{:S(2)}, u32[]{:S(2)}) collective-permute-start(bf16[8,192,256]{2,1,0:T(8,128)(2,1)} %get-tuple-element.38), channel_id=1, source_target_pairs={{0,24},{8,0},{16,8},{24,16},{32,56},{40,32},{48,40},{56,48},{64,88... | collective-permute-start | bytes 2359304 | tf_op jit(solution)/shard_map/ppermute | solution.py:561
  116.8 15.0 %copy-start.4 = (bf16[16,512]{1,0:T(8,128)(2,1)S(1)}, bf16[16,512]{1,0:T(8,128)(2,1)}, u32[]{:S(2)}) copy-start(bf16[16,512]{1,0:T(8,128)(2,1)} %get-tuple-element.21) | copy-start | bytes 49156
  116.9 14.9 %all-to-all-start.2 = ((f32[8,32,512]{2,1,0:T(8,128)}), f32[8,32,512]{2,1,0:T(8,128)S(1)}, u32[]{:S(2)}, u32[]{:S(2)}) async-start(f32[8,32,512]{2,1,0:T(8,128)} %project.1), calls=%async_computation.2 | async-start | bytes 1048576 | tf_op jit(solution)/shard_map/all_to_all | solution.py:606
